TPU v7x, 128 devices: a whole 4x4x4 slice. The times are simulated.
128 devices in a mesh: ctx: 32 (over x, y, core), ch: 4 (over z).
Axes of the slice: x: 4, y: 4, z: 4, core: 2. Of those that a mesh axis runs over, the one named last changes fastest.
Arguments:
- grad_out: bfloat16 [16384, 8192], P(('ctx', 'ch')), may hold values from -6 to 6
- query_medium: bfloat16 [16384, 8192], P('ctx', 'ch'), may hold values from -6 to 6
- key_medium: bfloat16 [16384, 8192], P('ctx', 'ch'), may hold values from -6 to 6
- value_medium: bfloat16 [16384, 8192], P('ctx', 'ch'), may hold values from -6 to 6
- query_modal: bfloat16 [16384, 8192], P('ctx', 'ch'), may hold values from -6 to 6
- key_modal: bfloat16 [16384, 8192], P('ctx', 'ch'), may hold values from -6 to 6
- medium_filter: bfloat16 [512, 128], P('ch'), may hold values from -0.5 to 0.5
- modal_decay: float32 [512, 16], P('ch'), may hold values from 0 to 1
- modal_residue: float32 [512, 16], P('ch'), may hold values from -1 to 1
Outputs:
- grad_query_medium: bfloat16 [16384, 8192], P(('ctx', 'ch'))
- grad_key_medium: bfloat16 [16384, 8192], P(('ctx', 'ch'))
- grad_value_medium: bfloat16 [16384, 8192], P(('ctx', 'ch'))
- grad_query_modal: bfloat16 [16384, 8192], P(('ctx', 'ch'))
- grad_key_modal: bfloat16 [16384, 8192], P(('ctx', 'ch'))
- grad_medium_filter: float32 [512, 128], P('ch')
All inputs are finite; a program needn't handle non-finite values.
Results may differ from a plain program's by a relative error of at most 0.015.
Values may be sent and summed in bfloat16 or wider, within the bound.
A program may use at most 192 MiB of HBM per device.

v0:
```python
import math

import jax
import jax.numpy as jnp
from jax import lax
from jax.sharding import PartitionSpec as P

GS = 16
TAPS = 128
NEAR = 128


highest = lax.Precision.HIGHEST


def shifted_2(block, axis, distance):
    devices = range(lax.axis_size(axis))
    route = [(i - distance, i) for i in devices if i - distance in devices]
    return lax.ppermute(block, axis, route)


def entering(value, axis, join, neutral, backward):
    count, mine = (lax.axis_size(axis), lax.axis_index(axis))
    pieces = jax.tree.map(lambda part: lax.all_gather(part, axis), value)
    if backward:
        pieces = jax.tree.map(lambda part: part[::-1], pieces)
        mine = count - 1 - mine
    subtotal = jax.tree.map(
        lambda part, zero: jnp.full_like(part, 0) + jnp.asarray(zero, part.dtype), value, neutral
    )

    def lap(position, subtotal):
        longer = join(subtotal, jax.tree.map(lambda part: part[position], pieces))
        return jax.tree.map(lambda new, old: jnp.where(position < mine, new, old), longer, subtotal)

    return lax.fori_loop(0, count - 1, lap, subtotal)


def skew_rows(vector, height):
    length = vector.shape[-1]
    leading = vector.shape[:-1]
    tiled_rows = jnp.broadcast_to(vector[..., None, :], leading + (height, length))
    tiled_rows = tiled_rows.reshape(leading + (height * length,))
    return tiled_rows[..., : height * (length - 1)].reshape(leading + (height, length - 1))


def medium_tables(medium_filter):
    groups = medium_filter.shape[0]
    tap_count = medium_filter.shape[1]
    front_zeros = jnp.zeros((groups, tap_count + 1), medium_filter.dtype)
    back_zeros = jnp.zeros((groups, tap_count), medium_filter.dtype)
    vector = jnp.concatenate([front_zeros, medium_filter[:, ::-1], back_zeros], axis=1)
    toeplitz = skew_rows(vector, tap_count)[:, :, tap_count:]
    return (toeplitz[:, :, :tap_count], toeplitz[:, :, tap_count:])


def near_table(near_taps):
    groups = near_taps.shape[0]
    count = near_taps.shape[1]
    front_zeros = jnp.zeros((groups, 1), near_taps.dtype)
    back_zeros = jnp.zeros((groups, count), near_taps.dtype)
    vector = jnp.concatenate([front_zeros, near_taps[:, ::-1], back_zeros], axis=1)
    return skew_rows(vector, count)[:, :, count:]


def diagonal_sums(products):
    groups, height, length = products.shape
    flat_values = products.reshape(groups, height * length)
    flat_values = jnp.concatenate(
        [flat_values, jnp.zeros((groups, height), products.dtype)], axis=1
    )
    shifted = flat_values.reshape(groups, height, length + 1)
    return jnp.sum(shifted[:, :, 1 : height + 1], axis=1)[:, ::-1]


def modal_tables(modal_decay, modal_residue):
    log_decay = jnp.log(modal_decay)
    lags = jnp.arange(NEAR).astype(jnp.float32)
    powers = jnp.exp(log_decay[:, :, None] * lags)
    taps_full = jnp.sum(modal_residue[:, :, None] * powers, axis=1)
    near_taps = taps_full.astype(jnp.bfloat16)
    end_weight = jnp.exp(log_decay[:, :, None] * (NEAR - 1 - lags))
    out_weight = modal_residue[:, :, None] * jnp.exp(log_decay[:, :, None] * (lags + 1.0))
    back_weight = modal_residue[:, :, None] * jnp.exp(log_decay[:, :, None] * (NEAR - lags))
    return (near_taps, end_weight, powers, out_weight, back_weight)


def column_blocks(values, height):
    return values.reshape(values.shape[0] // GS, GS, values.shape[1] // height, height)


def flat_columns(values):
    return values.reshape(values.shape[0] * values.shape[1], values.shape[2] * values.shape[3])


def state_groups(states):
    return states.reshape(states.shape[0], states.shape[1], states.shape[2] // GS, GS)


def state_rows(states):
    return states.reshape(states.shape[0], states.shape[1], states.shape[2] * states.shape[3])


def per_channel(group_rows):
    return jnp.repeat(group_rows.T, GS, axis=1)


def medium_apply(prev_tab, curr_tab, earlier_cols, current_cols):
    front_part = jnp.einsum(
        "gcbs,grs->gcbr",
        column_blocks(earlier_cols, TAPS),
        prev_tab,
        preferred_element_type=jnp.float32,
    )
    back_part = jnp.einsum(
        "gcbs,grs->gcbr",
        column_blocks(current_cols, TAPS),
        curr_tab,
        preferred_element_type=jnp.float32,
    )
    return flat_columns(front_part + back_part)


def medium_adjoint(prev_tab, curr_tab, current_grad, later_grad):
    own_part = jnp.einsum(
        "gcbr,grs->gcbs",
        column_blocks(current_grad, TAPS),
        curr_tab,
        preferred_element_type=jnp.float32,
    )
    next_part = jnp.einsum(
        "gcbr,grs->gcbs",
        column_blocks(later_grad, TAPS),
        prev_tab,
        preferred_element_type=jnp.float32,
    )
    return flat_columns(own_part + next_part)


def medium_products(grad_conv, earlier_cols, current_cols):
    grad_blocks = column_blocks(grad_conv, TAPS)
    front_part = jnp.einsum(
        "gcbr,gcbs->grs",
        grad_blocks,
        column_blocks(earlier_cols, TAPS),
        preferred_element_type=jnp.float32,
    )
    back_part = jnp.einsum(
        "gcbr,gcbs->grs",
        grad_blocks,
        column_blocks(current_cols, TAPS),
        preferred_element_type=jnp.float32,
    )
    return jnp.concatenate([front_part, back_part], axis=2)


def combine_states(earlier, later):
    return (earlier[0] * later[0], later[0] * earlier[1] + later[1])


def on_device(
    grad_out,
    query_medium,
    key_medium,
    value_medium,
    query_modal,
    key_modal,
    medium_filter,
    modal_decay,
    modal_residue,
):
    row_count = query_medium.shape[0]
    block_count = row_count // NEAR
    log_decay = jnp.log(modal_decay)
    cotangent = lax.all_to_all(grad_out, "ch", split_axis=1, concat_axis=0, tiled=True)
    query_cols = query_medium.T
    key_cols = key_medium.T
    value_cols = value_medium.T
    query_modal_cols = query_modal.T
    key_modal_cols = key_modal.T
    cotangent_cols = cotangent.T
    prev_tab, curr_tab = medium_tables(medium_filter)
    medium_input = (key_cols.astype(jnp.float32) * value_cols.astype(jnp.float32)).astype(
        jnp.bfloat16
    )
    tail_cols = shifted_2(medium_input[:, row_count - TAPS :], "ctx", 1)
    earlier_cols = jnp.concatenate([tail_cols, medium_input[:, : row_count - TAPS]], axis=1)
    medium_conv = medium_apply(prev_tab, curr_tab, earlier_cols, medium_input)
    medium_out = (query_cols.astype(jnp.float32) * medium_conv).astype(jnp.bfloat16)
    modal_input = (key_modal_cols.astype(jnp.float32) * medium_out.astype(jnp.float32)).astype(
        jnp.bfloat16
    )
    near_taps, end_weight, start_weight, out_weight, back_weight = modal_tables(
        modal_decay, modal_residue
    )
    near_tab = near_table(near_taps)
    input_blocks = column_blocks(modal_input, NEAR)
    end_states = state_rows(
        jnp.einsum(
            "gns,gcbs->bngc", end_weight, input_blocks.astype(jnp.float32), precision=highest
        )
    )
    log_rows = per_channel(log_decay)
    step_decay = jnp.exp(log_rows * NEAR)
    device_decay = jnp.exp(log_rows * row_count)
    own_total = jnp.zeros(end_states.shape[1:], jnp.float32)
    for block_id in range(block_count):
        own_total = step_decay * own_total + end_states[block_id]
    incoming = entering(
        (device_decay, own_total),
        "ctx",
        combine_states,
        (jnp.ones_like(device_decay), jnp.zeros_like(own_total)),
        False,
    )[1]
    carried = incoming
    before_list = []
    for block_id in range(block_count):
        before_list.append(carried)
        carried = step_decay * carried + end_states[block_id]
    befores = state_groups(jnp.stack(before_list))
    far_part = jnp.einsum("gnr,bngc->gcbr", out_weight, befores, precision=highest)
    near_part = jnp.einsum(
        "gcbs,grs->gcbr", input_blocks, near_tab, preferred_element_type=jnp.float32
    )
    modal_conv = flat_columns(near_part + far_part)
    grad_query_modal = (cotangent_cols.astype(jnp.float32) * modal_conv).astype(jnp.bfloat16)
    grad_modal_conv = (
        cotangent_cols.astype(jnp.float32) * query_modal_cols.astype(jnp.float32)
    ).astype(jnp.bfloat16)
    grad_blocks = column_blocks(grad_modal_conv, NEAR)
    start_states = state_rows(
        jnp.einsum(
            "gnr,gcbr->bngc", start_weight, grad_blocks.astype(jnp.float32), precision=highest
        )
    )
    own_adjoint = jnp.zeros(start_states.shape[1:], jnp.float32)
    for block_id in reversed(range(block_count)):
        own_adjoint = step_decay * own_adjoint + start_states[block_id]
    arriving = entering(
        (device_decay, own_adjoint),
        "ctx",
        combine_states,
        (jnp.ones_like(device_decay), jnp.zeros_like(own_adjoint)),
        True,
    )[1]
    carried = arriving
    next_list = [carried] * block_count
    for block_id in reversed(range(block_count)):
        next_list[block_id] = carried
        carried = step_decay * carried + start_states[block_id]
    nexts = state_groups(jnp.stack(next_list))
    near_back = jnp.einsum(
        "gcbr,grs->gcbs", grad_blocks, near_tab, preferred_element_type=jnp.float32
    )
    far_back = jnp.einsum("gns,bngc->gcbs", back_weight, nexts, precision=highest)
    grad_modal_input = flat_columns(near_back + far_back)
    grad_key_modal = (grad_modal_input * medium_out.astype(jnp.float32)).astype(jnp.bfloat16)
    grad_medium_out = grad_modal_input * key_modal_cols.astype(jnp.float32)
    grad_query_medium = (grad_medium_out * medium_conv).astype(jnp.bfloat16)
    grad_medium_conv = (grad_medium_out * query_cols.astype(jnp.float32)).astype(jnp.bfloat16)
    head_cols = shifted_2(grad_medium_conv[:, :TAPS], "ctx", -1)
    later_cols = jnp.concatenate([grad_medium_conv[:, TAPS:], head_cols], axis=1)
    grad_medium_input = medium_adjoint(prev_tab, curr_tab, grad_medium_conv, later_cols)
    grad_key_medium = (grad_medium_input * value_cols.astype(jnp.float32)).astype(jnp.bfloat16)
    grad_value_medium = (grad_medium_input * key_cols.astype(jnp.float32)).astype(jnp.bfloat16)
    products = medium_products(grad_medium_conv, earlier_cols, medium_input)
    filter_partial = diagonal_sums(products)
    filter_scale = 1.0 / math.sqrt(row_count * lax.axis_size("ctx") * GS)
    grad_medium_filter = lax.psum(filter_partial, "ctx") * filter_scale
    all_sent = (
        lax.all_to_all(grad_query_medium.T, "ch", split_axis=0, concat_axis=1, tiled=True),
        lax.all_to_all(grad_key_medium.T, "ch", split_axis=0, concat_axis=1, tiled=True),
        lax.all_to_all(grad_value_medium.T, "ch", split_axis=0, concat_axis=1, tiled=True),
        lax.all_to_all(grad_query_modal.T, "ch", split_axis=0, concat_axis=1, tiled=True),
        lax.all_to_all(grad_key_modal.T, "ch", split_axis=0, concat_axis=1, tiled=True),
    )
    return (all_sent[0], all_sent[1], all_sent[2], all_sent[3], all_sent[4], grad_medium_filter)


def solution(mesh):
    return jax.shard_map(
        on_device,
        mesh=mesh,
        in_specs=(
            P(("ctx", "ch"), None),
            P("ctx", "ch"),
            P("ctx", "ch"),
            P("ctx", "ch"),
            P("ctx", "ch"),
            P("ctx", "ch"),
            P("ch", None),
            P("ch", None),
            P("ch", None),
        ),
        out_specs=(
            P(("ctx", "ch"), None),
            P(("ctx", "ch"), None),
            P(("ctx", "ch"), None),
            P(("ctx", "ch"), None),
            P(("ctx", "ch"), None),
            P("ch", None),
        ),
        check_vma=False,
    )
```

profile of v0, /device:TPU:1, one launch (start us, length us, event | category | flops | bytes accessed | tf_op | source)
XLA Modules:
  0.0 622.6 jit_solution(16094387216456456437)
XLA Ops:
  13.6 5.8 all-to-all-start
  24.5 20.5 %all-to-all-done = bf16[128,4,2048]{0,2,1:T(8,128)(2,1)S(1)} async-done(((bf16[128,4,2048]{0,2,1:T(8,128)(2,1)}), bf16[128,4,2048]{0,2,1:T(8,128)(2,1)S(1)}, u32[]{:S(2)}, u32[]{:S(2)}) %all-to-all-start) | async-done | bytes 2097184 | tf_op jit(solution)/shard_map/all_to_all | solution.py:175
  79.1 5.3 collective-permute-start
  87.8 6.3 %broadcast_in_dim.17 = bf16[128,128,385]{0,2,1:T(8,128)(2,1)} broadcast(bf16[128,385]{0,1:T(8,128)(2,1)S(1)} %maximum_maximum_fusion), dimensions={0,2} | broadcast | bytes 12714240 | tf_op jit(solution)/shard_map/broadcast_in_dim | solution.py:42
  94.1 15.7 %reshape.282 = bf16[128,49280]{0,1:T(8,128)(2,1)} reshape(bf16[128,128,385]{0,2,1:T(8,128)(2,1)} %broadcast_in_dim.17) | data formatting | bytes 25231360 | tf_op jit(solution)/shard_map/reshape | solution.py:43
  123.9 4.5 broadcast_in_dim.13
  128.4 12.9 %reshape.278 = bf16[128,32896]{0,1:T(8,128)(2,1)} reshape(bf16[128,128,257]{0,2,1:T(8,128)(2,1)} %broadcast_in_dim.13) | data formatting | bytes 16842752 | tf_op jit(solution)/shard_map/reshape | solution.py:43
  147.0 6.7 %copy.322 = bf16[128,128,128]{2,1,0:T(8,128)(2,1)} copy(bf16[128,128,128]{0,2,1:T(8,128)(2,1)} %slice.90) | data formatting | bytes 8388608
  153.7 6.7 %copy.324 = bf16[128,128,128]{2,1,0:T(8,128)(2,1)} copy(bf16[128,128,128]{0,2,1:T(8,128)(2,1)} %get-tuple-element.277) | data formatting | bytes 8388608
  160.4 6.7 %copy.323 = bf16[128,128,128]{2,1,0:T(8,128)(2,1)} copy(bf16[128,128,128]{0,2,1:T(8,128)(2,1)} %get-tuple-element.276) | data formatting | bytes 8388608
  175.0 7.8 %fusion.37 = f32[128,16,4,128]{3,1,2,0:T(8,128)} fusion(bf16[128,128,128]{2,1,0:T(8,128)(2,1)} %copy.324, bf16[128,16,4,128]{3,2,1,0:T(4,128)(2,1)} %reshape.284), kind=kOutput, calls=%fused_computation.53 | convolution fusion | flops 268435456 | bytes 10485760 | tf_op jit(solution)/shard_map/gcbs,grs->gcbr/dot_general | solution.py:115
  189.5 7.0 %fusion.45 = f32[128,16,4,128]{3,1,2,0:T(8,128)S(1)} fusion(f32[128,16,4,128]{3,1,2,0:T(8,128)} %fusion.37, bf16[128,128,128]{2,1,0:T(8,128)(2,1)} %copy.323, bf16[128,16,4,128]{3,2,1,0:T(4,128)(2,1)} %reshape.281), kind=kOutput, calls=%fused_computation.65 | convolution fusion | flops 269484032 | bytes 14680064 | tf_op jit(solution)/shard_map/gcbs,grs->gcbr/dot_general | solution.py:109
  205.9 5.4 fusion.29
  211.3 4.7 rev.16
  216.0 4.7 rev.17
  220.8 33.9 %while.28 = (s32[]{:T(128)}, f32[16,2048]{1,0:T(8,128)S(1)}, s32[]{:T(128)}, f32[32,16,2048]{2,1,0:T(8,128)}, f32[32,16,2048]{2,1,0:T(8,128)}, /*index=5*/s32[]{:T(128)}, s32[]{:T(128)}) while((s32[]{:T(128)}, f32[16,2048]{1,0:T(8,128)S(1)}, s32[]{:T(128)}, f32[32,16,2048]{2,1,0:T(8,128)}, f32[32,16,2048]{2,1,0:T(8,128)}, ...), condition=%wide.region_2.3_spmd.clone, body=%wide.region_1.2_spmd.clone.sunk | while | flops 131076 | bytes 524397 | solution.py:36
  259.5 6.2 %bitcast_add_fusion.3 = f32[128,16,4,128]{3,1,2,0:T(8,128)S(1)} fusion(f32[128,16,4,128]{3,1,2,0:T(8,128)} %fusion.29, f32[1,16,128,16]{1,3,0,2:T(8,128)S(1)} %bitcast.301, f32[1,16,128,16]{1,3,0,2:T(8,128)S(1)} %bitcast.304, f32[1,16,128,16]{1,3,0,2:T(8,128)S(1)} %bitcast.305, f32[1,16,128,16]{1,3,0,2:T(8,128)} %bitcast.307, ...), kind=kOutput, calls=%fused_computation.59 | convolution fusion | flops 203292672 | bytes 8929792 | tf_op jit(solution)/shard_map/gns,bngc->gcbs/dot_general | solution.py:256
  269.3 5.8 fusion.55
  306.1 6.8 %fusion.27 = f32[128,16,4,128]{3,1,2,0:T(8,128)} fusion(bf16[128,128,128]{2,1,0:T(8,128)(2,1)S(1)} %copy-done, bf16[128,16,4,128]{3,2,1,0:T(4,128)(2,1)} %copy-done.2), kind=kOutput, calls=%fused_computation.43 | convolution fusion | flops 268435456 | bytes 10485760 | tf_op jit(solution)/shard_map/gcbs,grs->gcbr/dot_general | solution.py:223
  316.2 4.7 convolution_bitcast_fusion
  322.7 4.6 all-to-all-start.5
  327.4 6.4 %convolution_bitcast_fusion.1 = f32[128,128,128]{1,2,0:T(8,128)} fusion(bf16[128,16,4,128]{3,2,1,0:T(4,128)(2,1)} %reshape.281, bf16[128,16,4,128]{3,2,1,0:T(4,128)(2,1)S(1)} %reshape.286), kind=kOutput, calls=%fused_computation.62 | convolution fusion | flops 268435456 | bytes 12582912 | tf_op jit(solution)/shard_map/gcbr,gcbs->grs/dot_general | solution.py:142
  344.9 4.7 fusion.48
  360.5 33.9 %while.29 = (s32[]{:T(128)}, f32[16,2048]{1,0:T(8,128)S(1)}, s32[]{:T(128)}, f32[32,16,2048]{2,1,0:T(8,128)}, f32[32,16,2048]{2,1,0:T(8,128)}, /*index=5*/s32[]{:T(128)}, s32[]{:T(128)}) while((s32[]{:T(128)}, f32[16,2048]{1,0:T(8,128)S(1)}, s32[]{:T(128)}, f32[32,16,2048]{2,1,0:T(8,128)}, f32[32,16,2048]{2,1,0:T(8,128)}, ...), condition=%wide.region_4.5_spmd.clone, body=%wide.region_3.4_spmd.clone.sunk | while | flops 131076 | bytes 524397 | solution.py:36
  394.7 4.7 all-to-all-start.3
  407.8 6.6 %bitcast_add_fusion.2 = f32[128,16,4,128]{3,1,2,0:T(8,128)S(1)} fusion(f32[128,16,4,128]{3,1,2,0:T(8,128)} %fusion.27, f32[1,16,128,16]{1,3,0,2:T(8,128)} %bitcast.302, f32[1,16,128,16]{1,3,0,2:T(8,128)} %bitcast.303, f32[1,16,128,16]{1,3,0,2:T(8,128)} %bitcast.306, f32[1,16,128,16]{1,3,0,2:T(8,128)S(1)} %bitcast.300, f32[128]{0:T(128)S(1)} %broadcast_add_fusion, ...), kind=kOutput, calls=%fused_computation.42 | convolution fusion | flops 203292672 | bytes 8929792 | tf_op jit(solution)/shard_map/gnr,bngc->gcbr/dot_general | solution.py:222
  418.2 5.9 all-to-all-done.3
  428.6 11.7 %pad_maximum_fusion = f32[128,128,256]{1,2,0:T(8,128)} fusion(f32[128,128,128]{1,2,0:T(8,128)} %convolution_bitcast_fusion, f32[128,128,128]{1,2,0:T(8,128)} %convolution_bitcast_fusion.1), kind=kLoop, calls=%fused_computation.6 | loop fusion | flops 4194304 | bytes 33554432 | tf_op jit(solution)/shard_map/concatenate | solution.py:154
  440.3 17.6 %copy.296 = f32[128,128,256]{0,2,1:T(8,128)} copy(f32[128,128,256]{1,2,0:T(8,128)} %pad_maximum_fusion) | data formatting | bytes 33554432 | tf_op jit(solution)/shard_map/concatenate | solution.py:154
  458.0 13.3 %concatenate.25 = f32[128,32896]{0,1:T(8,128)} pad(f32[128,32768]{0,1:T(8,128)} %bitcast.275, f32[]{:T(128)} %constant.63.clone.1), padding=0_0x0_128 | pad | bytes 33619972 | tf_op jit(solution)/shard_map/concatenate | solution.py:69
  471.2 17.5 %reshape.292 = f32[128,128,257]{0,2,1:T(8,128)} reshape(f32[128,32896]{0,1:T(8,128)} %concatenate.25) | data formatting | bytes 33685504 | tf_op jit(solution)/shard_map/reshape | solution.py:72
  493.9 101.3 %all-reduce.3.cloned.1.call-done = f32[128,128]{0,1:T(8,128)} async-done(((f32[128,128]{0,1:T(8,128)}), f32[128,128]{0,1:T(8,128)}) %all-reduce.3.cloned.1.call-update) | async-done | bytes 65552 | tf_op jit(solution)/shard_map/psum | solution.py:270
  (237 shorter events, 268.2 us)
Async XLA Ops:
  7.2 204.1 %all-gather.4.cloned.1.call-start = ((), (), s32[]{:S(2)}) async-start(), calls=%async_computation.6 | async-start | bytes 4325376 | tf_op jit(solution)/shard_map/all_gather | solution.py:24
  13.6 31.3 %all-to-all-start = ((bf16[128,4,2048]{0,2,1:T(8,128)(2,1)}), bf16[128,4,2048]{0,2,1:T(8,128)(2,1)S(1)}, u32[]{:S(2)}, u32[]{:S(2)}) async-start(bf16[128,4,2048]{0,2,1:T(8,128)(2,1)} %bitcast.299), calls=%async_computation | async-start | bytes 4194304 | tf_op jit(solution)/shard_map/all_to_all | solution.py:175
  19.5 196.5 %all-gather.6.cloned.1.call-start = ((), (), s32[]{:S(2)}) async-start(), calls=%async_computation.7 | async-start | bytes 4325376 | tf_op jit(solution)/shard_map/all_gather | solution.py:24
  66.2 294.2 %all-gather.8.cloned.1.call-start = ((), (), s32[]{:S(2)}) async-start(), calls=%async_computation.8 | async-start | bytes 4325376 | tf_op jit(solution)/shard_map/all_gather | solution.py:24
  74.1 10.5 %copy-start.24 = (f32[128,16]{0,1:T(8,128)S(1)}, f32[128,16]{0,1:T(8,128)}, u32[]{:S(2)}) copy-start(f32[128,16]{0,1:T(8,128)} %param.21) | copy-start | bytes 24580
  74.1 11.9 %copy-start.23 = (bf16[128,128]{1,0:T(8,128)(2,1)S(1)}, bf16[128,128]{1,0:T(8,128)(2,1)}, u32[]{:S(2)}) copy-start(bf16[128,128]{1,0:T(8,128)(2,1)} %param.19) | copy-start | bytes 98308
  79.1 103.7 %collective-permute-start = (bf16[2048,128]{1,0:T(8,128)(2,1)}, bf16[2048,128]{1,0:T(8,128)(2,1)}, u32[]{:S(2)}, u32[]{:S(2)}) collective-permute-start(bf16[2048,128]{1,0:T(8,128)(2,1)} %slice.95), channel_id=1, source_target_pairs={{0,4},{4,8},{8,12},{12,16},{16,20},{20,24},{24,28},{28,32},{32,36}... | collective-permute-start | bytes 1572872 | tf_op jit(solution)/shard_map/ppermute | solution.py:19
  109.8 4.8 slice-start
  119.8 4.0 copy-start.21
  141.3 3.4 slice-start.1
  175.0 7.8 %slice-start.2 = ((bf16[2048,512]{1,0:T(8,128)(2,1)}), bf16[2048,384]{1,0:T(8,128)(2,1)S(1)}, s32[]{:S(2)}) async-start(bf16[2048,512]{1,0:T(8,128)(2,1)} %copy-done.4), calls=%async_computation.12 | async-start | bytes 3145728 | tf_op jit(solution)/shard_map/slice | solution.py:187
  196.6 8.4 %copy-start.11 = (f32[1,16,128,16]{1,3,0,2:T(8,128)S(1)}, f32[1,16,128,16]{1,3,0,2:T(8,128)}, u32[]{:S(2)}) copy-start(f32[1,16,128,16]{1,3,0,2:T(8,128)} %get-tuple-element.288) | copy-start | bytes 393220
  216.0 39.0 %copy-start.16 = (f32[16,2048]{1,0:T(8,128)S(1)}, f32[16,2048]{1,0:T(8,128)}, u32[]{:S(2)}) copy-start(f32[16,2048]{1,0:T(8,128)} %exp.58) | copy-start | bytes 393220
  216.0 39.0 %copy-start.18 = (f32[16,2048]{1,0:T(8,128)S(1)}, f32[16,2048]{1,0:T(8,128)}, u32[]{:S(2)}) copy-start(f32[16,2048]{1,0:T(8,128)} %copy.254) | copy-start | bytes 393220
  216.0 39.0 %copy-start.19 = (f32[16,2048]{1,0:T(8,128)S(1)}, f32[16,2048]{1,0:T(8,128)}, u32[]{:S(2)}) copy-start(f32[16,2048]{1,0:T(8,128)} %copy.253) | copy-start | bytes 393220
  216.0 39.0 %copy-start.20 = (f32[16,2048]{1,0:T(8,128)S(1)}, f32[16,2048]{1,0:T(8,128)}, u32[]{:S(2)}) copy-start(f32[16,2048]{1,0:T(8,128)} %copy.252) | copy-start | bytes 393220
  265.8 3.5 copy-start.14
  277.6 3.7 copy-start.2
  281.3 8.8 %copy-start.15 = (bf16[256,4,8,128]{3,2,1,0:T(8,128)(2,1)S(1)}, bf16[256,4,8,128]{3,2,1,0:T(8,128)(2,1)}, u32[]{:S(2)}) copy-start(bf16[256,4,8,128]{3,2,1,0:T(8,128)(2,1)} %get-tuple-element.279) | copy-start | bytes 6291460
  291.8 31.0 %all-to-all-start.1 = ((bf16[4,128,2048]{1,2,0:T(8,128)(2,1)}), bf16[4,128,2048]{1,2,0:T(8,128)(2,1)}, u32[]{:S(2)}, u32[]{:S(2)}) async-start(bf16[4,128,2048]{1,2,0:T(8,128)(2,1)} %bitcast.298), calls=%async_computation.1 | async-start | bytes 4194304 | tf_op jit(solution)/shard_map/all_to_all | solution.py:272
  298.8 7.3 %copy-start = (bf16[128,128,128]{2,1,0:T(8,128)(2,1)S(1)}, bf16[128,128,128]{2,1,0:T(8,128)(2,1)}, u32[]{:S(2)}) copy-start(bf16[128,128,128]{2,1,0:T(8,128)(2,1)} %copy.322) | copy-start | bytes 12582916
  300.9 38.4 %collective-permute-start.1 = (bf16[2048,128]{1,0:T(8,128)(2,1)}, bf16[2048,128]{1,0:T(8,128)(2,1)}, u32[]{:S(2)}, u32[]{:S(2)}) collective-permute-start(bf16[2048,128]{1,0:T(8,128)(2,1)} %slice.101), channel_id=1, source_target_pairs={{4,0},{8,4},{12,8},{16,12},{20,16},{24,20},{28,24},{32,28},{36,32}... | collective-permute-start | bytes 1572872 | tf_op jit(solution)/shard_map/ppermute | solution.py:19
  306.1 6.8 %copy-start.1 = (bf16[128,128,128]{2,1,0:T(8,128)(2,1)S(1)}, bf16[128,128,128]{2,1,0:T(8,128)(2,1)}, u32[]{:S(2)}) copy-start(bf16[128,128,128]{2,1,0:T(8,128)(2,1)} %copy.324) | copy-start | bytes 12582916
  312.9 3.3 copy-start.9
  322.7 33.5 %all-to-all-start.5 = ((bf16[4,128,2048]{1,2,0:T(8,128)(2,1)}), bf16[4,128,2048]{1,2,0:T(8,128)(2,1)}, u32[]{:S(2)}, u32[]{:S(2)}) async-start(bf16[4,128,2048]{1,2,0:T(8,128)(2,1)} %bitcast.297), calls=%async_computation.5 | async-start | bytes 4194304 | tf_op jit(solution)/shard_map/all_to_all | solution.py:276
  327.4 6.4 %copy-start.3 = (bf16[2048,512]{1,0:T(8,128)(2,1)S(1)}, bf16[2048,512]{1,0:T(8,128)(2,1)}, u32[]{:S(2)}) copy-start(bf16[2048,512]{1,0:T(8,128)(2,1)} %get-tuple-element.281) | copy-start | bytes 6291460
  333.8 3.5 copy-start.12
  356.3 38.4 %all-to-all-start.2 = ((bf16[4,128,2048]{1,2,0:T(8,128)(2,1)}), bf16[4,128,2048]{1,2,0:T(8,128)(2,1)S(1)}, u32[]{:S(2)}, u32[]{:S(2)}) async-start(bf16[4,128,2048]{1,2,0:T(8,128)(2,1)} %bitcast.296), calls=%async_computation.2 | async-start | bytes 4194304 | tf_op jit(solution)/shard_map/all_to_all | solution.py:273
  360.5 38.9 %copy-start.17 = (f32[16,2048]{1,0:T(8,128)S(1)}, f32[16,2048]{1,0:T(8,128)}, u32[]{:S(2)}) copy-start(f32[16,2048]{1,0:T(8,128)} %exp.58) | copy-start | bytes 393220
  394.7 29.4 %all-to-all-start.3 = ((bf16[4,128,2048]{1,2,0:T(8,128)(2,1)}), bf16[4,128,2048]{1,2,0:T(8,128)(2,1)}, u32[]{:S(2)}, u32[]{:S(2)}) async-start(bf16[4,128,2048]{1,2,0:T(8,128)(2,1)} %bitcast.295), calls=%async_computation.3 | async-start | bytes 4194304 | tf_op jit(solution)/shard_map/all_to_all | solution.py:274
  424.1 187.7 %all-to-all-start.4 = ((bf16[4,128,2048]{1,2,0:T(8,128)(2,1)}), bf16[4,128,2048]{1,2,0:T(8,128)(2,1)}, u32[]{:S(2)}, u32[]{:S(2)}) async-start(bf16[4,128,2048]{1,2,0:T(8,128)(2,1)} %copy_bitcast_fusion.1), calls=%async_computation.4 | async-start | bytes 4194304 | tf_op jit(solution)/shard_map/all_to_all | solution.py:275
  428.6 166.6 %all-reduce.3.cloned.1.call-start = ((), (), s32[]{:S(2)}) async-start(), calls=%async_computation.9 | async-start | bytes 131072 | tf_op jit(solution)/shard_map/psum | solution.py:270
  (8 other events, 14.9 us)
Sparse Core Ops, SparseCore 0:
  10.2 49.4 all-gather.3
  66.4 48.9 all-gather.5
  290.2 50.1 all-gather.7
  494.0 101.1 all-reduce.2
where the time goes:
time: 634 us; the launch traced here: 623 us
  local copies, waits for them, and re-layouts  266 us (42%)
  waiting for transfers between devices  130 us (21%)
  other arithmetic  113 us (18%)
  matrix products  62.8 us (10%)
  starting transfers between devices  35.6 us (6%)
  between operations  14.5 us (2%)
    psum x1, waiting for transfers between devices, on_device(): grad_medium_filter = lax.psum(filter_partial, 'ctx') * filter_scale  101 us
    unnamed x66, local copies, waits for them, and re-layouts  68.7 us
    select_n x62, other arithmetic, lap(): jnp.where(position < mine, new, old)  66.4 us
    reshape x2, local copies, waits for them, and re-layouts, skew_rows(): tiled_rows = tiled_rows.reshape(leading + (height * length,))  28.6 us
    all_to_all x1, waiting for transfers between devices, on_device(): lax.all_to_all(grad_out, 'ch', split_axis=1, concat_axis=0, tiled=True)  20.5 us
    reshape x6, local copies, waits for them, and re-layouts, column_blocks(): values.reshape(values.shape[0] // GS, GS, values.shape[1] // height, height)  18.3 us
    concatenate x1, local copies, waits for them, and re-layouts, medium_products(): return jnp.concatenate([front_part, back_part], axis=2)  17.6 us
    reshape x1, local copies, waits for them, and re-layouts, diagonal_sums(): shifted = flat_values.reshape(groups, height, length + 1)  17.5 us
  transfers between devices with their start and end apart: 12, of which 4 were waited for; matrix products, arithmetic and copies ran while one was open for 56% of the time, Pallas kernels for 0%

commit v1 on v0

v1 whole, which is shorter than its diff:
```python
import math

import jax
import jax.numpy as jnp
from jax import lax
from jax.experimental import pallas as pl
from jax.experimental.pallas import tpu as pltpu
from jax.sharding import PartitionSpec as P

GS = 16
TAPS = 128
NEAR = 128
LANES = 128
TILE_GROUPS = LANES // GS
MESH = pl.DeviceIdType.MESH

f32 = jnp.float32
bf16 = jnp.bfloat16


def dot(a, b):
    return jnp.dot(a, b, preferred_element_type=f32)


def lane_group(rows, columns):
    lane = lax.broadcasted_iota(jnp.int32, (rows, columns), 1)
    return jnp.bitwise_and(lax.shift_right_logical(lane, 4), TILE_GROUPS - 1)


def pick(stacked, rows, columns):
    group = lane_group(rows, columns)
    kept = stacked[0:rows]
    for g in range(1, TILE_GROUPS):
        kept = jnp.where(group == g, stacked[g * rows : (g + 1) * rows], kept)
    return kept


def skewed(row, height):
    wide = jnp.broadcast_to(row, (height, row.shape[1]))
    return pltpu.roll(wide, 0, 1, stride=1, stride_axis=0)


def split(value):
    high = value.astype(bf16)
    return high, (value - high.astype(f32)).astype(bf16)


def block_states(weight, data):
    high, low = split(weight)
    left = jnp.concatenate([high, low], axis=1)
    right = jnp.concatenate([data, data], axis=0)
    modes = weight.shape[0] // TILE_GROUPS
    return pick(dot(left, right), modes, data.shape[1])


def side_by_side(values, blocks):
    return jnp.concatenate([values[NEAR * b : NEAR * (b + 1)] for b in range(blocks)], axis=1)


def conv_pair(table_ref, data_ref, pair):
    low = 2 * pair * NEAR
    right = jnp.concatenate(
        [data_ref[low : low + 2 * NEAR], data_ref[low + NEAR : low + 3 * NEAR]], axis=1
    )
    return pick(dot(table_ref[...], right), NEAR, 2 * LANES)


def forward_kernel(
    key_ref, value_ref, query_ref, key_modal_ref, halo_ref, row_ref, log_ref, step_ref,
    conv_ref, out_ref, states_ref, total_ref, table_ref, data_ref,
):
    blocks = key_ref.shape[0] // NEAR
    for g in range(TILE_GROUPS):
        table_ref[NEAR * g : NEAR * (g + 1)] = skewed(row_ref[g : g + 1], NEAR).astype(bf16)
    data_ref[0:NEAR] = halo_ref[...]
    data_ref[NEAR:] = (key_ref[...].astype(f32) * value_ref[...].astype(f32)).astype(bf16)
    inputs = []
    for pair in range(blocks // 2):
        both = conv_pair(table_ref, data_ref, pair)
        for half in range(2):
            rows = slice(NEAR * (2 * pair + half), NEAR * (2 * pair + half + 1))
            conv = both[:, LANES * half : LANES * (half + 1)]
            conv_ref[rows] = conv
            out = (query_ref[rows].astype(f32) * conv).astype(bf16)
            out_ref[rows] = out
            inputs.append((key_modal_ref[rows].astype(f32) * out.astype(f32)).astype(bf16))
    lag = lax.broadcasted_iota(jnp.int32, (NEAR, NEAR), 1).astype(f32)
    weight = jnp.exp(log_ref[...] * (NEAR - 1 - lag))
    states = block_states(weight, jnp.concatenate(inputs, axis=1))
    total = jnp.zeros_like(total_ref)
    for b in range(blocks):
        state = states[:, LANES * b : LANES * (b + 1)]
        states_ref[b] = state
        total = step_ref[...] * total + state
    total_ref[...] = total


def adjoint_state_kernel(cotangent_ref, query_modal_ref, log_ref, step_ref, states_ref, total_ref):
    blocks = cotangent_ref.shape[0] // NEAR
    grad = (cotangent_ref[...].astype(f32) * query_modal_ref[...].astype(f32)).astype(bf16)
    lag = lax.broadcasted_iota(jnp.int32, (NEAR, NEAR), 1).astype(f32)
    states = block_states(jnp.exp(log_ref[...] * lag), side_by_side(grad, blocks))
    total = jnp.zeros_like(total_ref)
    for b in reversed(range(blocks)):
        state = states[:, LANES * b : LANES * (b + 1)]
        states_ref[b] = state
        total = step_ref[...] * total + state
    total_ref[...] = total


def fill_modal_table(table_ref, taps_ref, log_ref, residue_ref, adjoint):
    row = lax.broadcasted_iota(jnp.int32, (NEAR, LANES), 0)
    lane = lax.broadcasted_iota(jnp.int32, (NEAR, LANES), 1)
    near = row <= lane if adjoint else lane <= row
    lag = ((NEAR - row) if adjoint else (row + 1)).astype(f32)
    for g in range(TILE_GROUPS):
        taps = jnp.where(near, skewed(taps_ref[g : g + 1], NEAR), 0.0)
        far = residue_ref[g : g + 1] * jnp.exp(log_ref[g : g + 1] * lag)
        high = far.astype(bf16).astype(f32)
        far = jnp.where(lane < 32, high, far - high)
        rows = slice(NEAR * g, NEAR * (g + 1))
        table_ref[rows, 0:LANES] = taps.astype(bf16)
        table_ref[rows, LANES:] = far.astype(bf16)


def modal_blocks(table_ref, data_ref, states):
    high, low = split(states)
    modes = states.shape[0]
    data_ref[NEAR : NEAR + modes] = high
    data_ref[NEAR + modes : NEAR + 2 * modes] = low
    data_ref[NEAR + 2 * modes : NEAR + 3 * modes] = high
    data_ref[NEAR + 3 * modes :] = jnp.zeros(
        (NEAR - 3 * modes, data_ref.shape[1]), data_ref.dtype
    )
    parts = []
    for pair in range(data_ref.shape[1] // (2 * LANES)):
        right = data_ref[:, 2 * LANES * pair : 2 * LANES * (pair + 1)]
        both = pick(dot(table_ref[...], right), NEAR, 2 * LANES)
        parts += [both[:, 0:LANES], both[:, LANES:]]
    return parts


def modal_kernel(
    cotangent_ref, key_modal_ref, out_ref, states_ref, entering_ref, step_ref,
    taps_ref, log_ref, residue_ref, grad_ref, table_ref, data_ref,
):
    blocks = cotangent_ref.shape[0] // NEAR
    fill_modal_table(table_ref, taps_ref, log_ref, residue_ref, False)
    carried = entering_ref[...]
    befores = []
    for b in range(blocks):
        rows = slice(NEAR * b, NEAR * (b + 1))
        data_ref[0:NEAR, LANES * b : LANES * (b + 1)] = (
            key_modal_ref[rows].astype(f32) * out_ref[rows].astype(f32)
        ).astype(bf16)
        befores.append(carried)
        carried = step_ref[...] * carried + states_ref[b]
    parts = modal_blocks(table_ref, data_ref, jnp.concatenate(befores, axis=1))
    for b in range(blocks):
        rows = slice(NEAR * b, NEAR * (b + 1))
        grad_ref[rows] = (cotangent_ref[rows].astype(f32) * parts[b]).astype(bf16)


def modal_adjoint_kernel(
    cotangent_ref, query_modal_ref, key_modal_ref, query_ref, conv_ref, out_ref,
    states_ref, entering_ref, step_ref, taps_ref, log_ref, residue_ref,
    grad_key_modal_ref, grad_query_ref, grad_conv_ref, table_ref, data_ref,
):
    blocks = cotangent_ref.shape[0] // NEAR
    fill_modal_table(table_ref, taps_ref, log_ref, residue_ref, True)
    carried = entering_ref[...]
    nexts = [carried] * blocks
    for b in reversed(range(blocks)):
        rows = slice(NEAR * b, NEAR * (b + 1))
        data_ref[0:NEAR, LANES * b : LANES * (b + 1)] = (
            cotangent_ref[rows].astype(f32) * query_modal_ref[rows].astype(f32)
        ).astype(bf16)
        nexts[b] = carried
        carried = step_ref[...] * carried + states_ref[b]
    parts = modal_blocks(table_ref, data_ref, jnp.concatenate(nexts, axis=1))
    for b in range(blocks):
        rows = slice(NEAR * b, NEAR * (b + 1))
        grad_key_modal_ref[rows] = (parts[b] * out_ref[rows].astype(f32)).astype(bf16)
        grad_out = parts[b] * key_modal_ref[rows].astype(f32)
        grad_query_ref[rows] = (grad_out * conv_ref[rows]).astype(bf16)
        grad_conv_ref[rows] = (grad_out * query_ref[rows].astype(f32)).astype(bf16)


def medium_adjoint_kernel(
    grad_ref, halo_ref, key_ref, value_ref, row_ref,
    grad_key_ref, grad_value_ref, table_ref, data_ref,
):
    blocks = grad_ref.shape[0] // NEAR
    for g in range(TILE_GROUPS):
        table_ref[NEAR * g : NEAR * (g + 1)] = skewed(row_ref[g : g + 1], NEAR).astype(bf16)
    data_ref[0 : NEAR * blocks] = grad_ref[...]
    data_ref[NEAR * blocks :] = halo_ref[...]
    for pair in range(blocks // 2):
        both = conv_pair(table_ref, data_ref, pair)
        for half in range(2):
            rows = slice(NEAR * (2 * pair + half), NEAR * (2 * pair + half + 1))
            grad_input = both[:, LANES * half : LANES * (half + 1)]
            grad_key_ref[rows] = (grad_input * value_ref[rows].astype(f32)).astype(bf16)
            grad_value_ref[rows] = (grad_input * key_ref[rows].astype(f32)).astype(bf16)


def product_kernel(grad_ref, key_ref, value_ref, halo_ref, sums_ref, left_ref, data_ref):
    blocks = grad_ref.shape[0] // NEAR
    data_ref[0:NEAR] = halo_ref[...]
    data_ref[NEAR:] = (key_ref[...].astype(f32) * value_ref[...].astype(f32)).astype(bf16)
    row = lax.broadcasted_iota(jnp.int32, (NEAR, NEAR), 0)
    lane = lax.broadcasted_iota(jnp.int32, (NEAR, NEAR), 1)
    flip = jnp.where(row + lane == NEAR - 1, 1.0, 0.0).astype(bf16)
    flipped = dot(flip, side_by_side(grad_ref[...], blocks))
    group = lane_group(NEAR, blocks * LANES)
    for g in range(TILE_GROUPS):
        left_ref[NEAR * g : NEAR * (g + 1)] = jnp.where(group == g, flipped, 0.0).astype(bf16)
    right = jnp.concatenate(
        [data_ref[NEAR * b : NEAR * (b + 2)] for b in range(blocks)], axis=1
    )
    products = lax.dot_general(
        left_ref[...], right, (((1,), (1,)), ((), ())), preferred_element_type=f32
    )
    for g in range(TILE_GROUPS):
        turned = pltpu.roll(
            products[NEAR * g : NEAR * (g + 1)], 0, 1, stride=1, stride_axis=0
        )
        sums_ref[g : g + 1] = jnp.sum(turned[:, NEAR:], axis=0, keepdims=True)


def join_kernel(grid, total_ref, adjoint_ref, log_ref, entering_ref, arriving_ref,
                slots, pair_ref, send_sem, recv_sem):
    size_x, size_y, _ = grid
    me = lax.axis_index("ctx")
    core = lax.rem(me, 2)
    y = lax.rem(lax.div(me, 2), size_y)
    x = lax.div(me, 2 * size_y)

    def index(a, b, c):
        return (a * size_y + b) * 2 + c

    partner = index(x, y, 1 - core)
    y_peers = [index(x, lax.rem(y + k, size_y), core) for k in range(1, size_y)]
    x_peers = [index(lax.rem(x + k, size_x), y, core) for k in range(1, size_x)]
    peers = [partner] + y_peers + x_peers
    barrier = pltpu.get_barrier_semaphore()
    for peer in peers:
        pl.semaphore_signal(barrier, inc=1, device_id={"ctx": peer}, device_id_type=MESH)
    pl.semaphore_wait(barrier, len(peers))

    def send(source, target, slot, peer):
        copy = pltpu.make_async_remote_copy(
            src_ref=source, dst_ref=target, send_sem=send_sem.at[slot],
            recv_sem=recv_sem.at[slot], device_id={"ctx": peer}, device_id_type=MESH,
        )
        copy.start()
        return copy

    log = log_ref[...]
    rows = log_ref.shape

    def decay(steps):
        return jnp.where(steps == 0, 1.0, jnp.exp(log * (steps * 1.0)))

    span = TAPS * 4
    first = send(total_ref, pair_ref.at[0], 0, partner)
    second = send(adjoint_ref, pair_ref.at[1], 1, partner)
    one = jnp.exp(log * span)
    first.wait()
    second.wait()
    forward = core == 0
    mine = jnp.where(forward, total_ref[...], adjoint_ref[...])
    theirs = jnp.where(forward, pair_ref[0], pair_ref[1])
    slots[0] = one * mine + theirs

    def stage(base, peers, place, count, chip_steps):
        copies = [
            send(slots.at[base], slots.at[base + k + 1], 2 + base + k, peer)
            for k, peer in enumerate(peers)
        ]
        for copy in copies:
            copy.wait()
        before = jnp.zeros(rows, f32)
        whole = jnp.zeros(rows, f32)
        for k in range(count):
            source = lax.rem(place - k + count, count)
            value = slots[base + k]
            gap = jnp.where(forward, place - source - 1, source - place - 1)
            rest = jnp.where(forward, count - 1 - source, source)
            near = gap >= 0
            weight = decay(jnp.where(near, gap, 0) * (chip_steps * 2 * span))
            before = before + jnp.where(near, weight * value, 0.0)
            whole = whole + decay(rest * (chip_steps * 2 * span)) * value
        return before, whole

    before_y, whole_y = stage(0, y_peers, y, size_y, 1)
    slots[size_y] = whole_y
    before_x, _ = stage(size_y, x_peers, x, size_x, size_y)
    inner = jnp.where(forward, y, size_y - 1 - y)
    before = before_y + decay(inner * (2 * span)) * before_x
    pair_ref[2] = before
    last = send(pair_ref.at[2], pair_ref.at[3], 2 + size_x + size_y, partner)
    last.wait()
    other = pair_ref[3]
    entering_ref[...] = jnp.where(forward, before, one * other + pair_ref[0])
    arriving_ref[...] = jnp.where(forward, one * other + pair_ref[1], before)


def tile_spec(rows):
    return pl.BlockSpec((rows, LANES), lambda i: (0, i))


def group_spec(columns):
    return pl.BlockSpec((TILE_GROUPS, columns), lambda i: (i, 0))


def call(body, tiles, in_specs, outs, out_specs, scratch, flops, *args):
    moved = sum(math.prod(a.shape) * a.dtype.itemsize for a in list(args) + list(outs))
    return pl.pallas_call(
        body,
        grid=(tiles,),
        in_specs=in_specs,
        out_shape=outs,
        out_specs=out_specs,
        scratch_shapes=scratch,
        cost_estimate=pl.CostEstimate(flops=flops, bytes_accessed=moved, transcendentals=0),
    )(*args)


def on_device(
    sizes,
    grad_out,
    query_medium,
    key_medium,
    value_medium,
    query_modal,
    key_modal,
    medium_filter,
    modal_decay,
    modal_residue,
):
    row_count, channels = query_medium.shape
    blocks = row_count // NEAR
    tiles = channels // LANES
    groups, modes = modal_decay.shape
    devices = lax.axis_size("ctx")
    data = jax.ShapeDtypeStruct((row_count, channels), bf16)
    data32 = jax.ShapeDtypeStruct((row_count, channels), f32)
    states_shape = jax.ShapeDtypeStruct((blocks, modes, channels), f32)
    state_shape = jax.ShapeDtypeStruct((modes, channels), f32)
    column = tile_spec(row_count)
    halo = tile_spec(NEAR)
    state = tile_spec(modes)
    states = pl.BlockSpec((blocks, modes, LANES), lambda i: (0, 0, i))
    log_block = pl.BlockSpec((TILE_GROUPS * modes, NEAR), lambda i: (i, 0))
    wide_table = pltpu.VMEM((TILE_GROUPS * NEAR, 2 * NEAR), bf16)
    long_data = pltpu.VMEM((row_count + NEAR, LANES), bf16)
    wide_data = pltpu.VMEM((2 * NEAR, blocks * LANES), bf16)
    work = 2 * tiles * TILE_GROUPS * NEAR * 2 * NEAR * blocks * LANES

    cotangent = lax.all_to_all(grad_out, "ch", split_axis=1, concat_axis=0, tiled=True)

    tail = (
        key_medium[row_count - TAPS :].astype(f32) * value_medium[row_count - TAPS :].astype(f32)
    ).astype(bf16)
    tail = lax.ppermute(tail, "ctx", [(i, i + 1) for i in range(devices - 1)])

    filter32 = medium_filter.astype(f32)
    no_taps = jnp.zeros_like(filter32)
    forward_row = jnp.concatenate(
        [no_taps[:, :1], filter32[:, ::-1], no_taps[:, : TAPS - 1]], axis=1
    )
    adjoint_row = jnp.concatenate([filter32, no_taps], axis=1)
    log_decay = jnp.log(modal_decay)
    lags = jnp.arange(NEAR).astype(f32)
    taps = jnp.sum(modal_residue[:, :, None] * jnp.exp(log_decay[:, :, None] * lags), axis=1)
    taps = taps.astype(bf16).astype(f32)
    taps_back = jnp.concatenate([taps[:, :1], taps[:, :0:-1]], axis=1)
    log_columns = jnp.broadcast_to(log_decay.reshape(groups * modes, 1), (groups * modes, NEAR))

    def three(value):
        return jnp.concatenate([value] * 3 + [jnp.zeros((groups, LANES - 3 * modes), f32)], axis=1)

    log_three, residue_three = three(log_decay), three(modal_residue)
    log_rows = jnp.repeat(log_decay.T, GS, axis=1)
    step = jnp.exp(log_rows * NEAR)

    conv, medium_out, end_states, own_total = call(
        forward_kernel, tiles,
        [column] * 4 + [halo, group_spec(2 * TAPS), log_block, state],
        (data32, data, states_shape, state_shape), (column, column, states, state),
        [wide_table, long_data], work,
        key_medium, value_medium, query_medium, key_modal, tail, forward_row, log_columns, step,
    )
    start_states, own_adjoint = call(
        adjoint_state_kernel, tiles, [column] * 2 + [log_block, state],
        (states_shape, state_shape), (states, state), [], work // 8,
        cotangent, query_modal, log_columns, step,
    )
    size_x, size_y, _ = sizes
    vmem = pl.BlockSpec(memory_space=pltpu.VMEM)
    entering, arriving = pl.pallas_call(
        lambda *refs: join_kernel(sizes, *refs),
        in_specs=[vmem] * 3,
        out_shape=(state_shape, state_shape),
        out_specs=(vmem, vmem),
        scratch_shapes=[
            pltpu.VMEM((size_x + size_y, modes, channels), f32),
            pltpu.VMEM((4, modes, channels), f32),
            pltpu.SemaphoreType.DMA((3 + size_x + size_y,)),
            pltpu.SemaphoreType.DMA((3 + size_x + size_y,)),
        ],
        compiler_params=pltpu.CompilerParams(collective_id=0, has_side_effects=True),
    )(own_total, own_adjoint, log_rows)

    modal_specs = [states, state, state, group_spec(NEAR), group_spec(LANES), group_spec(LANES)]
    (grad_query_modal,) = call(
        modal_kernel, tiles, [column] * 3 + modal_specs, (data,), (column,),
        [wide_table, wide_data], work,
        cotangent, key_modal, medium_out, end_states, entering, step,
        taps_back, log_three, residue_three,
    )

    def home(value):
        return lax.all_to_all(value, "ch", split_axis=0, concat_axis=1, tiled=True)

    grad_query_modal = home(grad_query_modal)
    grad_key_modal, grad_query, grad_conv = call(
        modal_adjoint_kernel, tiles, [column] * 6 + modal_specs, (data,) * 3, (column,) * 3,
        [wide_table, wide_data], work,
        cotangent, query_modal, key_modal, query_medium, conv, medium_out,
        start_states, arriving, step, taps, log_three, residue_three,
    )
    head = lax.ppermute(grad_conv[:TAPS], "ctx", [(i + 1, i) for i in range(devices - 1)])
    grad_key_modal = home(grad_key_modal)
    grad_query = home(grad_query)
    (sums,) = call(
        product_kernel, tiles, [column] * 3 + [halo],
        (jax.ShapeDtypeStruct((groups, NEAR), f32),), (group_spec(NEAR),),
        [pltpu.VMEM((TILE_GROUPS * NEAR, blocks * LANES), bf16), long_data], work,
        grad_conv, key_medium, value_medium, tail,
    )
    grad_key, grad_value = call(
        medium_adjoint_kernel, tiles,
        [column, halo, column, column, group_spec(2 * TAPS)],
        (data, data), (column, column), [wide_table, long_data], work,
        grad_conv, head, key_medium, value_medium, adjoint_row,
    )
    filter_scale = 1.0 / math.sqrt(row_count * devices * GS)
    grad_filter = lax.psum(sums[:, ::-1], "ctx") * filter_scale
    return (grad_query, home(grad_key), home(grad_value), grad_query_modal, grad_key_modal,
            grad_filter)


def solution(mesh):
    count = mesh.shape["ctx"] // 2
    side = math.isqrt(count)
    sizes = (side, count // side, 2)

    def body(*args):
        return on_device(sizes, *args)

    rows = P(("ctx", "ch"), None)
    groups = P("ch", None)
    return jax.shard_map(
        body,
        mesh=mesh,
        in_specs=(rows,) + (P("ctx", "ch"),) * 5 + (groups,) * 3,
        out_specs=(rows,) * 5 + (groups,),
        check_vma=False,
    )
```

time: 634 us -> 368 us (0.58); the launches traced: 623 us -> 365 us
  local copies, waits for them, and re-layouts: 266 us -> 24.1 us
  Pallas kernels: 0 us -> 114 us
  other arithmetic: 113 us -> 7.19 us
  matrix products: 62.8 us -> 0 us
  blocking collectives: 0 us -> 61 us
  waiting for transfers between devices: 130 us -> 117 us
  starting transfers between devices: 35.6 us -> 27.1 us
    pallas_call x0 -> x7, Pallas kernels: none -> 114 us  [the longest x6 89.1 us: call(): pl.pallas_call(body, grid=(tiles,), in_specs=in_specs, out_shape=outs, ou...]
    select_n x62 -> x0, other arithmetic: 66.4 us -> none  [lap(): jnp.where(position < mine, new, old)]
    unnamed x66 -> x16, local copies, waits for them, and re-layouts: 68.7 us -> 2.33 us
    reshape x9 -> x1, local copies, waits for them, and re-layouts: 64.4 us -> 0.63 us  [on_device(): log_rows = jnp.repeat(log_decay.T, GS, axis=1)]
    dot_general x12 -> x0, matrix products: 62.8 us -> none  [the longest x1 7.84 us: medium_apply(): jnp.einsum('gcbs,grs->gcbr', column_blocks(current_cols, TAPS), curr_tab,...]
    all_to_all x0 -> x2, blocking collectives: none -> 61 us  [home(): return lax.all_to_all(value, 'ch', split_axis=0, concat_axis=1, tiled=True)]
    concatenate x7 -> x4, local copies, waits for them, and re-layouts: 31.2 us -> 0.82 us  [the longest x1 0.66 us: on_device(): adjoint_row = jnp.concatenate([filter32, no_taps], axis=1)]
    squeeze x14 -> x0, local copies, waits for them, and re-layouts: 24.6 us -> none  [the longest x7 13.5 us: on_device(): own_adjoint = step_decay * own_adjoint + start_states[block_id]]
  transfers between devices with their start and end apart: 12 -> 7, of which waited for: 4 -> 4; matrix products, arithmetic and copies ran while one was open for 56% -> 7% of each run, Pallas kernels for 0% -> 17%
where the time goes in v1:
time: 368 us; the launch traced here: 365 us
  waiting for transfers between devices  117 us (32%)
  Pallas kernels  114 us (31%)
  blocking collectives  61 us (17%)
  starting transfers between devices  27.1 us (7%)
  local copies, waits for them, and re-layouts  24.1 us (7%)
  between operations  14.2 us (4%)
  other arithmetic  7.19 us (2%)
    psum x1, waiting for transfers between devices, on_device(): grad_filter = lax.psum(sums[:, ::-1], 'ctx') * filter_scale  96.5 us
    pallas_call x6, Pallas kernels, call(): pl.pallas_call(body, grid=(tiles,), in_specs=in_specs, out_shape=outs, ou...  89.1 us
    all_to_all x2, blocking collectives, home(): return lax.all_to_all(value, 'ch', split_axis=0, concat_axis=1, tiled=True)  61 us
    pallas_call x1, Pallas kernels, on_device(): pl.pallas_call(lambda *refs: join_kernel(sizes, *refs), in_specs=[vmem] *...  24.9 us
    all_to_all x3, starting transfers between devices, home(): return lax.all_to_all(value, 'ch', split_axis=0, concat_axis=1, tiled=True)  13.4 us
    all_to_all x5, local copies, waits for them, and re-layouts, home(): return lax.all_to_all(value, 'ch', split_axis=0, concat_axis=1, tiled=True)  12.5 us
    all_to_all x3, waiting for transfers between devices, home(): return lax.all_to_all(value, 'ch', split_axis=0, concat_axis=1, tiled=True)  10.6 us
  transfers between devices with their start and end apart: 7, of which 4 were waited for; matrix products, arithmetic and copies ran while one was open for 7% of the time, Pallas kernels for 17%

profile of v1, /device:TPU:1, one launch (start us, length us, event | category | flops | bytes accessed | tf_op | source)
XLA Modules:
  0.0 364.6 jit_solution(13627569269520347965)
XLA Ops:
  7.2 2.1 multiply_convert_fusion
  9.3 4.6 %collective-permute-start = (bf16[128,2048]{1,0:T(8,128)(2,1)}, bf16[128,2048]{1,0:T(8,128)(2,1)}, u32[]{:S(2)}, u32[]{:S(2)}) collective-permute-start(bf16[128,2048]{1,0:T(8,128)(2,1)} %multiply_convert_fusion), channel_id=1, source_target_pairs={{0,4},{4,8},{8,12},{12,16},{16,20},{20,24},{24,28},{28,32},{32,36}... | collective-permute-start | bytes 1572872 | tf_op jit(solution)/shard_map/ppermute | solution.py:366
  13.9 3.2 copy.58
  17.0 5.2 %all-to-all-start = ((bf16[128,4,2048]{2,0,1:T(8,128)(2,1)}), bf16[128,4,2048]{2,0,1:T(8,128)(2,1)S(1)}, u32[]{:S(2)}, u32[]{:S(2)}) async-start(bf16[128,4,2048]{2,0,1:T(8,128)(2,1)} %bitcast.29), calls=%async_computation | async-start | bytes 4194304 | tf_op jit(solution)/shard_map/all_to_all | solution.py:361
  23.5 0.8 maximum_maximum_fusion.2
  27.6 1.3 broadcast_in_dim.7.log_ref
  28.9 16.3 %shard_map.136 = (f32[512,2048]{1,0:T(8,128)}, bf16[512,2048]{1,0:T(8,128)(2,1)}, f32[4,16,2048]{2,1,0:T(8,128)}, f32[16,2048]{1,0:T(8,128)}) custom-call(bf16[512,2048]{1,0:T(8,128)(2,1)} %key_ref.5, bf16[512,2048]{1,0:T(8,128)(2,1)} %value_ref.5, bf16[512,2048]{1,0:T(8,128)(2,1)} %query_ref.3, bf16[512,2048]{1,0:T(8,128)(2,1)} %key_modal_ref.5, ...), custom_call_target="tpu_custom_call" | custom-call | flops 4294967296 | bytes 17170432 | tf_op jit(solution)/shard_map/pallas_call | solution.py:319
  45.1 3.7 %all-to-all-done = bf16[128,4,2048]{2,0,1:T(8,128)(2,1)S(1)} async-done(((bf16[128,4,2048]{2,0,1:T(8,128)(2,1)}), bf16[128,4,2048]{2,0,1:T(8,128)(2,1)S(1)}, u32[]{:S(2)}, u32[]{:S(2)}) %all-to-all-start) | async-done | bytes 2097184 | tf_op jit(solution)/shard_map/all_to_all | solution.py:361
  48.8 1.3 copy-done.1
  50.2 11.1 %shard_map.137 = (f32[4,16,2048]{2,1,0:T(8,128)}, f32[16,2048]{1,0:T(8,128)}) custom-call(bf16[512,2048]{1,0:T(8,128)(2,1)} %bitcast.32, bf16[512,2048]{1,0:T(8,128)(2,1)} %query_modal_ref.3, f32[2048,128]{1,0:T(8,128)} %broadcast_in_dim.7.log_ref, f32[16,2048]{1,0:T(8,128)} %multiply_exponential_fusion.step_ref), custom_call_target="tpu_custom_call" | custom-call | flops 536870912 | bytes 6029312 | tf_op jit(solution)/shard_map/pallas_call | solution.py:319
  61.3 24.9 %shard_map.138 = (f32[16,2048]{1,0:T(8,128)}, f32[16,2048]{1,0:T(8,128)}) custom-call(f32[16,2048]{1,0:T(8,128)} %get-tuple-element.22.refs_0_, f32[16,2048]{1,0:T(8,128)} %get-tuple-element.23.refs_1_, f32[16,2048]{1,0:T(8,128)} %copy-done.2), custom_call_target="tpu_custom_call" | custom-call | tf_op jit(solution)/shard_map/pallas_call | solution.py:402
  86.2 17.4 %shard_map.139 = (bf16[512,2048]{1,0:T(8,128)(2,1)}, bf16[512,2048]{1,0:T(8,128)(2,1)}, bf16[512,2048]{1,0:T(8,128)(2,1)}) custom-call(bf16[512,2048]{1,0:T(8,128)(2,1)} %bitcast.33, bf16[512,2048]{1,0:T(8,128)(2,1)} %query_modal_ref.3, bf16[512,2048]{1,0:T(8,128)(2,1)} %key_modal_ref.5, bf16[512,2048]{1,0:T(8,128)(2,1)} %query_ref.3, ...), custom_call_target="tpu_custom_call" | custom-call | flops 4294967296 | bytes 21954560 | tf_op jit(solution)/shard_map/pallas_call | solution.py:319
  103.6 29.7 %all_to_all.114 = bf16[4,128,2048]{2,1,0:T(8,128)(2,1)S(1)} all-to-all(bf16[4,128,2048]{2,1,0:T(8,128)(2,1)} %bitcast.45), channel_id=1, replica_groups=mesh['ctx'=32,'ch'=4] {'ch'}, dimensions={0} | all-to-all | bytes 4194304 | tf_op jit(solution)/shard_map/all_to_all | solution.py:425
  133.3 4.5 %all-to-all-start.1 = ((bf16[4,128,2048]{2,1,0:T(8,128)(2,1)}), bf16[4,128,2048]{2,1,0:T(8,128)(2,1)}, u32[]{:S(2)}, u32[]{:S(2)}) async-start(bf16[4,128,2048]{2,1,0:T(8,128)(2,1)} %bitcast.38), calls=%async_computation.1 | async-start | bytes 4194304 | tf_op jit(solution)/shard_map/all_to_all | solution.py:425
  137.8 14.7 %shard_map.141 = bf16[512,2048]{1,0:T(8,128)(2,1)} custom-call(bf16[512,2048]{1,0:T(8,128)(2,1)} %bitcast.34, bf16[512,2048]{1,0:T(8,128)(2,1)} %key_modal_ref.5, bf16[512,2048]{1,0:T(8,128)(2,1)} %get-tuple-element.20.out_ref, f32[4,16,2048]{2,1,0:T(8,128)} %get-tuple-element.29.states_ref, f32[16,2048]{1,0:T(8,128)} %get-tuple-element.30.entering_ref, ...), custom_call_target="tpu_custom_call" | custom-call | flops 4294967296 | bytes 9371648 | tf_op jit(solution)/shard_map/pallas_call | solution.py:319
  152.5 10.6 %all-to-all-done.1 = bf16[4,128,2048]{2,1,0:T(8,128)(2,1)} async-done(((bf16[4,128,2048]{2,1,0:T(8,128)(2,1)}), bf16[4,128,2048]{2,1,0:T(8,128)(2,1)}, u32[]{:S(2)}, u32[]{:S(2)}) %all-to-all-start.1) | async-done | bytes 2097184 | tf_op jit(solution)/shard_map/all_to_all | solution.py:425
  163.1 4.4 %all-to-all-start.4 = ((bf16[4,128,2048]{2,1,0:T(8,128)(2,1)}), bf16[4,128,2048]{2,1,0:T(8,128)(2,1)}, u32[]{:S(2)}, u32[]{:S(2)}) async-start(bf16[4,128,2048]{2,1,0:T(8,128)(2,1)} %bitcast.37), calls=%async_computation.4 | async-start | bytes 4194304 | tf_op jit(solution)/shard_map/all_to_all | solution.py:425
  167.5 1.1 slice.25
  168.6 4.0 %collective-permute-start.1 = (bf16[128,2048]{1,0:T(8,128)(2,1)S(1)}, bf16[128,2048]{1,0:T(8,128)(2,1)S(1)}, u32[]{:S(2)}, u32[]{:S(2)}) collective-permute-start(bf16[128,2048]{1,0:T(8,128)(2,1)S(1)} %slice.25), channel_id=1, source_target_pairs={{4,0},{8,4},{12,8},{16,12},{20,16},{24,20},{28,24},{32,28},{36,32}... | collective-permute-start | bytes 1572872 | tf_op jit(solution)/shard_map/ppermute | solution.py:434
  173.2 6.3 %collective-permute-done.1.halo_ref = bf16[128,2048]{1,0:T(8,128)(2,1)S(1)} collective-permute-done((bf16[128,2048]{1,0:T(8,128)(2,1)S(1)}, bf16[128,2048]{1,0:T(8,128)(2,1)S(1)}, u32[]{:S(2)}, u32[]{:S(2)}) %collective-permute-start.1) | collective-permute-done | bytes 524320 | tf_op jit(solution)/shard_map/ppermute | solution.py:434
  180.3 14.7 %shard_map.140 = (bf16[512,2048]{1,0:T(8,128)(2,1)}, bf16[512,2048]{1,0:T(8,128)(2,1)}) custom-call(bf16[512,2048]{1,0:T(8,128)(2,1)} %get-tuple-element.26.grad_ref, bf16[128,2048]{1,0:T(8,128)(2,1)} %copy-done.6, bf16[512,2048]{1,0:T(8,128)(2,1)} %key_ref.5, bf16[512,2048]{1,0:T(8,128)(2,1)} %value_ref.5, f32[128,256]{1,0:T(8,128)} %concatenate.18.row_ref), custom_call_target="tpu_custom_call" | custom-call | flops 4294967296 | bytes 11141120 | tf_op jit(solution)/shard_map/pallas_call | solution.py:319
  195.1 31.3 %all_to_all.115 = bf16[4,128,2048]{2,1,0:T(8,128)(2,1)} all-to-all(bf16[4,128,2048]{2,1,0:T(8,128)(2,1)} %bitcast.44), channel_id=1, replica_groups=mesh['ctx'=32,'ch'=4] {'ch'}, dimensions={0} | all-to-all | bytes 4194304 | tf_op jit(solution)/shard_map/all_to_all | solution.py:425
  226.4 4.5 %all-to-all-start.2 = ((bf16[4,128,2048]{2,1,0:T(8,128)(2,1)}), bf16[4,128,2048]{2,1,0:T(8,128)(2,1)}, u32[]{:S(2)}, u32[]{:S(2)}) async-start(bf16[4,128,2048]{2,1,0:T(8,128)(2,1)} %bitcast.36), calls=%async_computation.2 | async-start | bytes 4194304 | tf_op jit(solution)/shard_map/all_to_all | solution.py:425
  230.9 14.9 %shard_map.142 = f32[128,128]{1,0:T(8,128)} custom-call(bf16[512,2048]{1,0:T(8,128)(2,1)} %get-tuple-element.26.grad_ref, bf16[512,2048]{1,0:T(8,128)(2,1)} %key_ref.5, bf16[512,2048]{1,0:T(8,128)(2,1)} %value_ref.5, bf16[128,2048]{1,0:T(8,128)(2,1)} %collective-permute-done.halo_ref), custom_call_target="tpu_custom_call" | custom-call | flops 4294967296 | bytes 6881280 | tf_op jit(solution)/shard_map/pallas_call | solution.py:319
  245.7 1.6 rev.11
  247.3 96.5 %all-reduce.3.cloned.1.call-done = f32[128,128]{1,0:T(8,128)} async-done(((f32[128,128]{1,0:T(8,128)}), f32[128,128]{1,0:T(8,128)}) %all-reduce.3.cloned.1.call-update) | async-done | bytes 65552 | tf_op jit(solution)/shard_map/psum | solution.py:450
  343.8 1.5 broadcast_multiply_fusion
  345.3 1.5 copy.56
  346.7 3.2 copy.52
  349.9 3.3 copy.55
  353.2 1.5 copy.54
  354.6 3.2 copy.53
  (40 shorter events, 6.0 us)
Async XLA Ops:
  9.3 18.3 %collective-permute-start = (bf16[128,2048]{1,0:T(8,128)(2,1)}, bf16[128,2048]{1,0:T(8,128)(2,1)}, u32[]{:S(2)}, u32[]{:S(2)}) collective-permute-start(bf16[128,2048]{1,0:T(8,128)(2,1)} %multiply_convert_fusion), channel_id=1, source_target_pairs={{0,4},{4,8},{8,12},{12,16},{16,20},{20,24},{24,28},{28,32},{32,36}... | collective-permute-start | bytes 1572872 | tf_op jit(solution)/shard_map/ppermute | solution.py:366
  17.0 5.2 %copy-start.4 = (f32[128,16]{0,1:T(8,128)S(1)}, f32[128,16]{0,1:T(8,128)}, u32[]{:S(2)}) copy-start(f32[128,16]{0,1:T(8,128)} %param.17) | copy-start | bytes 24580
  17.0 5.3 %copy-start.5 = (f32[128,16]{0,1:T(8,128)S(1)}, f32[128,16]{0,1:T(8,128)}, u32[]{:S(2)}) copy-start(f32[128,16]{0,1:T(8,128)} %param.16) | copy-start | bytes 24580
  17.0 6.3 %copy-start.3 = (bf16[128,128]{1,0:T(8,128)(2,1)S(1)}, bf16[128,128]{1,0:T(8,128)(2,1)}, u32[]{:S(2)}) copy-start(bf16[128,128]{1,0:T(8,128)(2,1)} %param.15) | copy-start | bytes 98308
  17.0 31.8 %all-to-all-start = ((bf16[128,4,2048]{2,0,1:T(8,128)(2,1)}), bf16[128,4,2048]{2,0,1:T(8,128)(2,1)S(1)}, u32[]{:S(2)}, u32[]{:S(2)}) async-start(bf16[128,4,2048]{2,0,1:T(8,128)(2,1)} %bitcast.29), calls=%async_computation | async-start | bytes 4194304 | tf_op jit(solution)/shard_map/all_to_all | solution.py:361
  26.8 18.3 %copy-start.2 = (f32[16,2048]{1,0:T(8,128)}, f32[16,2048]{1,0:T(8,128)S(1)}, u32[]{:S(2)}) copy-start(f32[16,2048]{1,0:T(8,128)S(1)} %reshape.41.refs_2_) | copy-start | bytes 393220
  48.8 1.3 copy-start.1
  133.3 29.8 %all-to-all-start.1 = ((bf16[4,128,2048]{2,1,0:T(8,128)(2,1)}), bf16[4,128,2048]{2,1,0:T(8,128)(2,1)}, u32[]{:S(2)}, u32[]{:S(2)}) async-start(bf16[4,128,2048]{2,1,0:T(8,128)(2,1)} %bitcast.38), calls=%async_computation.1 | async-start | bytes 4194304 | tf_op jit(solution)/shard_map/all_to_all | solution.py:425
  163.1 32.0 %all-to-all-start.4 = ((bf16[4,128,2048]{2,1,0:T(8,128)(2,1)}), bf16[4,128,2048]{2,1,0:T(8,128)(2,1)}, u32[]{:S(2)}, u32[]{:S(2)}) async-start(bf16[4,128,2048]{2,1,0:T(8,128)(2,1)} %bitcast.37), calls=%async_computation.4 | async-start | bytes 4194304 | tf_op jit(solution)/shard_map/all_to_all | solution.py:425
  168.6 10.9 %collective-permute-start.1 = (bf16[128,2048]{1,0:T(8,128)(2,1)S(1)}, bf16[128,2048]{1,0:T(8,128)(2,1)S(1)}, u32[]{:S(2)}, u32[]{:S(2)}) collective-permute-start(bf16[128,2048]{1,0:T(8,128)(2,1)S(1)} %slice.25), channel_id=1, source_target_pairs={{4,0},{8,4},{12,8},{16,12},{20,16},{24,20},{28,24},{32,28},{36,32}... | collective-permute-start | bytes 1572872 | tf_op jit(solution)/shard_map/ppermute | solution.py:434
  179.5 0.8 copy-start.6
  226.4 128.3 %all-to-all-start.2 = ((bf16[4,128,2048]{2,1,0:T(8,128)(2,1)}), bf16[4,128,2048]{2,1,0:T(8,128)(2,1)}, u32[]{:S(2)}, u32[]{:S(2)}) async-start(bf16[4,128,2048]{2,1,0:T(8,128)(2,1)} %bitcast.36), calls=%async_computation.2 | async-start | bytes 4194304 | tf_op jit(solution)/shard_map/all_to_all | solution.py:425
  230.8 113.0 %all-reduce.3.cloned.1.call-start = ((), (), s32[]{:S(2)}) async-start(), calls=%async_computation.6 | async-start | bytes 131072 | tf_op jit(solution)/shard_map/psum | solution.py:450
  349.9 3.3 copy-start
Sparse Core Ops, SparseCore 0:
  247.4 96.2 all-reduce.2

commit v2 on v0

v2 whole, which is shorter than its diff:
```python
import math

import jax
import jax.numpy as jnp
from jax import lax
from jax.experimental import pallas as pl
from jax.experimental.pallas import tpu as pltpu
from jax.sharding import PartitionSpec as P

GS = 16
TAPS = 128
NEAR = 128
LANES = 128
TILE_GROUPS = LANES // GS
CHUNKS = 4
MESH = pl.DeviceIdType.MESH

f32 = jnp.float32
bf16 = jnp.bfloat16
highest = lax.Precision.HIGHEST


def dot(a, b):
    return jnp.dot(a, b, preferred_element_type=f32)


def iota(shape, axis):
    return lax.broadcasted_iota(jnp.int32, shape, axis)


def ramp(axis):
    return iota((NEAR, LANES), axis)


def lane_group(rows, columns):
    lane = iota((rows, columns), 1)
    return jnp.bitwise_and(lax.shift_right_logical(lane, 4), TILE_GROUPS - 1)


def pick(stacked, rows, columns):
    group = lane_group(rows, columns)
    kept = stacked[0:rows]
    for g in range(1, TILE_GROUPS):
        kept = jnp.where(group == g, stacked[g * rows : (g + 1) * rows], kept)
    return kept


def skewed(row, height):
    wide = jnp.broadcast_to(row, (height, row.shape[1]))
    return pltpu.roll(wide, 0, 1, stride=1, stride_axis=0)


def split(value):
    high = value.astype(bf16)
    return high, (value - high.astype(f32)).astype(bf16)


def product(a, b):
    return (a.astype(f32) * b.astype(f32)).astype(bf16)


def block_rows(b):
    return slice(NEAR * b, NEAR * (b + 1))


def block_states(weight, data):
    high, low = split(weight.T)
    left = jnp.concatenate([high, low], axis=1)
    right = jnp.concatenate([data, data], axis=0)
    return pick(dot(left, right), weight.shape[1] // TILE_GROUPS, data.shape[1])


def fill_medium_table(table_ref, row_ref, tile):
    rows = row_ref[pl.ds(pl.multiple_of(tile * TILE_GROUPS, TILE_GROUPS), TILE_GROUPS)]
    for g in range(TILE_GROUPS):
        table_ref[block_rows(g)] = skewed(rows[g : g + 1], NEAR).astype(bf16)


def medium_pair(table_ref, data_ref, lanes, pair):
    low = 2 * pair * NEAR
    right = jnp.concatenate(
        [data_ref[low : low + 2 * NEAR, lanes], data_ref[low + NEAR : low + 3 * NEAR, lanes]],
        axis=1,
    )
    return pick(dot(table_ref[...], right), NEAR, 2 * LANES)


def fill_modal_table(table_ref, log_row, residue_row, modes, adjoint):
    row, lane = ramp(0), ramp(1)
    lag = row if adjoint else jnp.bitwise_and(NEAR - row, NEAR - 1)
    terms = residue_row * jnp.exp(log_row * lag.astype(f32))
    member = jnp.where(lane_group(TILE_GROUPS, LANES) == iota((TILE_GROUPS, LANES), 0), 1.0, 0.0)
    taps = lax.dot_general(
        member, terms, (((1,), (1,)), ((), ())), precision=highest, preferred_element_type=f32
    )
    small = iota((TILE_GROUPS, LANES), 1)

    def three(value):
        turned = pltpu.roll(
            jnp.broadcast_to(value, (TILE_GROUPS, LANES)), 0, 1, stride=modes, stride_axis=0
        )
        again, third = pltpu.roll(turned, modes, 1), pltpu.roll(turned, 2 * modes, 1)
        return jnp.where(small < modes, turned, jnp.where(small < 2 * modes, again, third))

    logs, residues = three(log_row), jnp.where(small < 3 * modes, three(residue_row), 0.0)
    near = row <= lane if adjoint else lane <= row
    far_lag = ((NEAR - row) if adjoint else (row + 1)).astype(f32)
    for g in range(TILE_GROUPS):
        q = (TILE_GROUPS - g) % TILE_GROUPS
        table_ref[block_rows(g), 0:LANES] = jnp.where(
            near, skewed(taps[g : g + 1], NEAR), 0.0
        ).astype(bf16)
        far = residues[q : q + 1] * jnp.exp(logs[q : q + 1] * far_lag)
        high = far.astype(bf16).astype(f32)
        table_ref[block_rows(g), LANES:] = jnp.where(
            lane < 2 * modes, high, far - high
        ).astype(bf16)


def modal_blocks(table_ref, data_ref, states):
    high, low = split(states)
    modes = states.shape[0]
    data_ref[NEAR : NEAR + modes] = high
    data_ref[NEAR + modes : NEAR + 2 * modes] = low
    data_ref[NEAR + 2 * modes : NEAR + 3 * modes] = high
    parts = []
    for pair in range(data_ref.shape[1] // (2 * LANES)):
        right = data_ref[:, 2 * LANES * pair : 2 * LANES * (pair + 1)]
        both = pick(dot(table_ref[...], right), NEAR, 2 * LANES)
        parts += [both[:, 0:LANES], both[:, LANES:]]
    return parts


class Place:
    def __init__(self, sizes):
        self.size_x, self.size_y, _ = sizes
        self.me = lax.axis_index("ctx")
        self.core = lax.rem(self.me, 2)
        self.y = lax.rem(lax.div(self.me, 2), self.size_y)
        self.x = lax.div(self.me, 2 * self.size_y)
        self.partner = self.index(self.x, self.y, 1 - self.core)
        self.y_peers = [
            self.index(self.x, lax.rem(self.y + k, self.size_y), self.core)
            for k in range(1, self.size_y)
        ]
        self.x_peers = [
            self.index(lax.rem(self.x + k, self.size_x), self.y, self.core)
            for k in range(1, self.size_x)
        ]

    def index(self, x, y, core):
        return (x * self.size_y + y) * 2 + core


def remote(source, target, sems, slot, peer):
    return pltpu.make_async_remote_copy(
        src_ref=source, dst_ref=target, send_sem=sems[0].at[slot], recv_sem=sems[1].at[slot],
        device_id=peer, device_id_type=MESH,
    )


def gather(buffer, place, peers, sems, base):
    copies = [
        remote(buffer.at[place], buffer.at[place], sems, base + k, {"ctx": peer})
        for k, peer in enumerate(peers)
    ]
    for copy in copies:
        copy.start()
    return copies


def finish(copies):
    for copy in copies:
        copy.wait()


class Join:
    def __init__(self, place, forward, total_ref, result_ref, log_ref, pair, by_y, by_x, out, sems):
        self.place, self.forward = place, forward
        self.total, self.result, self.log = total_ref, result_ref, log_ref
        self.pair, self.by_y, self.by_x, self.out, self.sems = pair, by_y, by_x, out, sems
        half = total_ref.shape[1] // 2
        self.mine = pl.ds(pl.multiple_of(place.core * half, half), half)
        self.other = pl.ds(pl.multiple_of((1 - place.core) * half, half), half)
        self.span = 4 * NEAR

    def decay(self, steps):
        return jnp.exp(self.log[:, self.mine] * (steps * 1.0))

    def start(self):
        place = self.place
        self.copies = [
            remote(self.total.at[:, self.other], self.pair.at[place.core], self.sems, 0,
                   {"ctx": place.partner})
        ]
        self.copies[0].start()
        self.pair[place.core] = self.total[:, self.mine]

    def along_y(self):
        finish(self.copies)
        first, second = (0, 1) if self.forward else (1, 0)
        chip = self.decay(self.span) * self.pair[first] + self.pair[second]
        self.by_y[self.place.y] = chip
        self.copies = gather(self.by_y, self.place.y, self.place.y_peers, self.sems, 1)

    def walk(self, buffer, count, here, decay):
        before = jnp.zeros(buffer.shape[1:], f32)
        whole = before
        for s in range(count) if self.forward else reversed(range(count)):
            value = buffer[s]
            earlier = (s < here) if self.forward else (s > here)
            before = jnp.where(earlier, decay * before + value, before)
            whole = decay * whole + value
        return before, whole

    def along_x(self):
        finish(self.copies)
        place = self.place
        self.before, whole = self.walk(self.by_y, place.size_y, place.y, self.decay(2 * self.span))
        self.out[1] = self.before
        self.by_x[place.x] = whole
        self.copies = gather(self.by_x, place.x, place.x_peers, self.sems, place.size_y)

    def share(self):
        finish(self.copies)
        place = self.place
        chip = self.decay(2 * self.span)
        before, _ = self.walk(
            self.by_x, place.size_x, place.x, self.decay(2 * self.span * place.size_y)
        )
        inner = place.y if self.forward else place.size_y - 1 - place.y
        for k in range(place.size_y - 1):
            before = jnp.where(k < inner, chip * before, before)
        near = self.out[1] + before
        first = 0 if self.forward else 1
        far = self.decay(self.span) * near + self.pair[first]
        is_first = place.core == first
        self.result[:, self.mine] = jnp.where(is_first, near, far)
        self.out[0] = jnp.where(is_first, far, near)
        self.copies = [
            remote(self.out.at[0], self.result.at[:, self.mine], self.sems,
                   place.size_y + place.size_x - 1, {"ctx": place.partner})
        ]
        self.copies[0].start()

    def end(self):
        finish(self.copies)


def whole_kernel(
    sizes, scale,
    cotangent_in, query_in, key_in, value_in, query_modal_in, key_modal_in,
    filter_ref, decay_ref, residue_ref,
    out0, out1, out2, out3, out4, filter_out,
    query, key, value, query_modal, key_modal, cotangent,
    medium_input, conv, medium_out, grad_conv,
    stage0, stage1, stage2, stage3, stage4,
    end_states, start_states, own_total, own_adjoint, entering, arriving, log_rows,
    pair_f, y_f, x_f, o_f, pair_b, y_b, x_b, o_b,
    forward_row, adjoint_row, table, wide, left, sums, core_sums, y_sums, x_sums,
    load_sem, cot_send, cot_recv, tail_send, tail_recv, head_send, head_recv,
    join_send, join_recv, back_send, back_recv, sum_send, sum_recv,
    out_send, out_recv, own_sem,
):
    place = Place(sizes)
    me, z = place.me, lax.axis_index("ch")
    size_z = lax.axis_size("ch")
    devices = lax.axis_size("ctx")
    row_count, channels = query.shape
    blocks = row_count // NEAR
    tiles = channels // LANES
    modes = own_total.shape[0]
    part = channels // CHUNKS
    following = lax.rem(me + 1, devices)
    previous = lax.rem(me + devices - 1, devices)

    def columns(chunk):
        return pl.ds(chunk * part, part)

    loads = [
        pltpu.make_async_copy(source, target, load_sem.at[n])
        for n, (source, target) in enumerate(
            [(key_in, key), (value_in, value), (query_in, query), (key_modal_in, key_modal),
             (query_modal_in, query_modal)]
        )
    ]
    for copy in loads:
        copy.start()

    z_peers = [lax.rem(z + k, size_z) for k in range(1, size_z)]
    barrier = pltpu.get_barrier_semaphore()
    for peer in z_peers:
        pl.semaphore_signal(barrier, inc=1, device_id={"ch": peer}, device_id_type=MESH)
    ring = [place.partner] + place.y_peers + place.x_peers + [following, previous]
    for peer in ring:
        pl.semaphore_signal(barrier, inc=1, device_id={"ctx": peer}, device_id_type=MESH)
    pl.semaphore_wait(barrier, len(z_peers) + len(ring))

    own_rows = pl.ds(pl.multiple_of(z * NEAR, NEAR), NEAR)
    own_columns = pl.ds(pl.multiple_of(z * channels, channels), channels)

    cot_copies = []
    for chunk in range(CHUNKS):
        for k, peer in enumerate(z_peers):
            source = pl.ds(pl.multiple_of(peer * channels + chunk * part, part), part)
            copy = remote(
                cotangent_in.at[:, source], cotangent.at[own_rows, columns(chunk)],
                (cot_send.at[k], cot_recv.at[k]), chunk, {"ch": peer},
            )
            copy.start()
            cot_copies.append(copy)
    cot_own = pltpu.make_async_copy(
        cotangent_in.at[:, own_columns], cotangent.at[own_rows], own_sem.at[5]
    )
    cot_own.start()

    loads[0].wait()
    loads[1].wait()
    last = slice(row_count - TAPS, row_count)
    medium_input[row_count:] = product(key[last], value[last])
    tail_copies = [
        remote(
            medium_input.at[pl.ds(row_count, TAPS), columns(c)],
            medium_input.at[pl.ds(0, TAPS), columns(c)],
            (tail_send, tail_recv), c, {"ctx": following},
        )
        for c in range(CHUNKS)
    ]
    for copy in tail_copies:
        copy.start()

    taps_in = filter_ref[...]
    turn = jnp.where(
        iota((TAPS, 2 * TAPS), 0) + iota((TAPS, 2 * TAPS), 1) == TAPS, 1.0, 0.0
    ).astype(bf16)
    forward_row[...] = dot(taps_in, turn)
    adjoint_row[:, 0:TAPS] = taps_in.astype(f32)
    adjoint_row[:, TAPS:] = jnp.zeros(taps_in.shape, f32)
    wide[NEAR + 3 * modes :] = jnp.zeros((NEAR - 3 * modes, wide.shape[1]), bf16)
    spread = jnp.where(
        lax.shift_right_logical(ramp(0), 4) == lax.shift_right_logical(ramp(1), 4), 1.0, 0.0
    )
    own_mode = jnp.bitwise_and(iota((modes, LANES), 1), modes - 1) == iota((modes, LANES), 0)

    def lanes_of(tile):
        return pl.ds(pl.multiple_of(tile * LANES, LANES), LANES)

    @pl.loop(0, tiles)
    def _(tile):
        kept = jnp.where(own_mode, decay_ref[pl.ds(tile, 1)], 0.0)
        log_rows[:, lanes_of(tile)] = jnp.log(
            jnp.dot(kept, spread, precision=highest, preferred_element_type=f32)
        )

    loads[2].wait()
    loads[3].wait()
    early = slice(0, row_count - TAPS)

    for chunk in range(CHUNKS):
        tail_copies[chunk].wait_recv()

        @pl.when(me == 0)
        def _():
            medium_input[0:TAPS, columns(chunk)] = jnp.zeros((TAPS, part), bf16)

        @pl.loop(chunk * tiles // CHUNKS, (chunk + 1) * tiles // CHUNKS)
        def _(tile):
            lanes = lanes_of(tile)
            medium_input[TAPS:row_count, lanes] = product(key[early, lanes], value[early, lanes])
            fill_medium_table(table, forward_row, tile)
            inputs = []
            for pair in range(blocks // 2):
                both = medium_pair(table, medium_input, lanes, pair)
                for half in range(2):
                    rows = block_rows(2 * pair + half)
                    part_conv = both[:, LANES * half : LANES * (half + 1)]
                    conv[rows, lanes] = part_conv
                    out = (query[rows, lanes].astype(f32) * part_conv).astype(bf16)
                    medium_out[rows, lanes] = out
                    inputs.append(product(key_modal[rows, lanes], out))
            log_row = jnp.log(decay_ref[pl.ds(tile, 1)])
            weight = jnp.exp(log_row * (NEAR - 1 - ramp(0)).astype(f32))
            states = block_states(weight, jnp.concatenate(inputs, axis=1))
            step = jnp.exp(log_rows[:, lanes] * NEAR)
            total = jnp.zeros((modes, LANES), f32)
            for b in range(blocks):
                state = states[:, LANES * b : LANES * (b + 1)]
                end_states[b, :, lanes] = state
                total = step * total + state
            own_total[:, lanes] = total

    forward = Join(place, True, own_total, entering, log_rows, pair_f, y_f, x_f, o_f,
                   (join_send, join_recv))
    backward = Join(place, False, own_adjoint, arriving, log_rows, pair_b, y_b, x_b, o_b,
                    (back_send, back_recv))
    forward.start()
    cot_own.wait()
    loads[4].wait()
    forward.along_y()

    def adjoint_states(chunk):
        for copy in cot_copies[(size_z - 1) * chunk : (size_z - 1) * (chunk + 1)]:
            copy.wait_recv()

        @pl.loop(chunk * tiles // CHUNKS, (chunk + 1) * tiles // CHUNKS)
        def _(tile):
            lanes = lanes_of(tile)
            grads = jnp.concatenate(
                [product(cotangent[block_rows(b), lanes], query_modal[block_rows(b), lanes])
                 for b in range(blocks)],
                axis=1,
            )
            log_row = jnp.log(decay_ref[pl.ds(tile, 1)])
            states = block_states(jnp.exp(log_row * ramp(0).astype(f32)), grads)
            step = jnp.exp(log_rows[:, lanes] * NEAR)
            total = jnp.zeros((modes, LANES), f32)
            for b in reversed(range(blocks)):
                state = states[:, LANES * b : LANES * (b + 1)]
                start_states[b, :, lanes] = state
                total = step * total + state
            own_adjoint[:, lanes] = total

    adjoint_states(0)
    adjoint_states(1)
    forward.along_x()
    adjoint_states(2)
    adjoint_states(3)
    forward.share()
    backward.start()
    forward.end()

    out_copies, own_copies = [], []

    def send_home(n, stage, out, chunk):
        for k, peer in enumerate(z_peers):
            rows = pl.ds(pl.multiple_of(peer * NEAR, NEAR), NEAR)
            target = pl.ds(pl.multiple_of(z * channels + chunk * part, part), part)
            copy = remote(
                stage.at[rows, columns(chunk)], out.at[:, target],
                (out_send.at[n, k], out_recv.at[n, k]), chunk, {"ch": peer},
            )
            copy.start()
            out_copies.append(copy)
        if chunk == CHUNKS - 1:
            copy = pltpu.make_async_copy(
                stage.at[own_rows], out.at[:, own_columns], own_sem.at[n]
            )
            copy.start()
            own_copies.append(copy)

    for chunk in range(CHUNKS):

        @pl.loop(chunk * tiles // CHUNKS, (chunk + 1) * tiles // CHUNKS)
        def _(tile):
            lanes = lanes_of(tile)
            log_row = jnp.log(decay_ref[pl.ds(tile, 1)])
            fill_modal_table(table, log_row, residue_ref[pl.ds(tile, 1)], modes, False)
            step = jnp.exp(log_rows[:, lanes] * NEAR)
            carried = entering[:, lanes]
            befores = []
            for b in range(blocks):
                wide[0:NEAR, LANES * b : LANES * (b + 1)] = product(
                    key_modal[block_rows(b), lanes], medium_out[block_rows(b), lanes]
                )
                befores.append(carried)
                carried = step * carried + end_states[b, :, lanes]
            parts = modal_blocks(table, wide, jnp.concatenate(befores, axis=1))
            for b in range(blocks):
                rows = block_rows(b)
                stage3[rows, lanes] = (cotangent[rows, lanes].astype(f32) * parts[b]).astype(bf16)

        send_home(3, stage3, out3, chunk)
        if chunk == 0:
            backward.along_y()
        if chunk == 1:
            backward.along_x()
        if chunk == 2:
            backward.share()
    backward.end()

    head_copies = []
    for chunk in range(CHUNKS):

        @pl.loop(chunk * tiles // CHUNKS, (chunk + 1) * tiles // CHUNKS)
        def _(tile):
            lanes = lanes_of(tile)
            log_row = jnp.log(decay_ref[pl.ds(tile, 1)])
            fill_modal_table(table, log_row, residue_ref[pl.ds(tile, 1)], modes, True)
            step = jnp.exp(log_rows[:, lanes] * NEAR)
            carried = arriving[:, lanes]
            nexts = [carried] * blocks
            for b in reversed(range(blocks)):
                wide[0:NEAR, LANES * b : LANES * (b + 1)] = product(
                    cotangent[block_rows(b), lanes], query_modal[block_rows(b), lanes]
                )
                nexts[b] = carried
                carried = step * carried + start_states[b, :, lanes]
            parts = modal_blocks(table, wide, jnp.concatenate(nexts, axis=1))
            for b in range(blocks):
                rows = block_rows(b)
                stage4[rows, lanes] = (parts[b] * medium_out[rows, lanes].astype(f32)).astype(bf16)
                grad_out = parts[b] * key_modal[rows, lanes].astype(f32)
                stage0[rows, lanes] = (grad_out * conv[rows, lanes]).astype(bf16)
                grad_conv[rows, lanes] = (grad_out * query[rows, lanes].astype(f32)).astype(bf16)

        copy = remote(
            grad_conv.at[pl.ds(0, TAPS), columns(chunk)],
            grad_conv.at[pl.ds(row_count, TAPS), columns(chunk)],
            (head_send, head_recv), chunk, {"ctx": previous},
        )
        copy.start()
        head_copies.append(copy)
        send_home(4, stage4, out4, chunk)
        send_home(0, stage0, out0, chunk)

    flip = jnp.where(ramp(0) + ramp(1) == NEAR - 1, 1.0, 0.0)

    @pl.loop(0, tiles)
    def _(tile):
        lanes = lanes_of(tile)
        grads = jnp.concatenate([grad_conv[block_rows(b), lanes] for b in range(blocks)], axis=1)
        flipped = dot(flip.astype(bf16), grads)
        group = lane_group(NEAR, blocks * LANES)
        for g in range(TILE_GROUPS):
            left[block_rows(g)] = jnp.where(group == g, flipped, 0.0).astype(bf16)
        right = jnp.concatenate(
            [medium_input[NEAR * b : NEAR * (b + 2), lanes] for b in range(blocks)], axis=1
        )
        products = lax.dot_general(
            left[...], right, (((1,), (1,)), ((), ())), preferred_element_type=f32
        )
        rows = []
        for g in range(TILE_GROUPS):
            turned = pltpu.roll(products[block_rows(g)], 0, 1, stride=1, stride_axis=0)
            rows.append(jnp.sum(turned[:, NEAR:], axis=0, keepdims=True))
        sums[pl.ds(pl.multiple_of(tile * TILE_GROUPS, TILE_GROUPS), TILE_GROUPS)] = (
            jnp.concatenate(rows, axis=0)
        )

    core_sums[place.core] = sums[...]
    sum_sems = (sum_send, sum_recv)
    sum_copies = gather(core_sums, place.core, [place.partner], sum_sems, 0)

    for chunk in range(CHUNKS):
        head_copies[chunk].wait_recv()

        @pl.when(me == devices - 1)
        def _():
            grad_conv[row_count:, columns(chunk)] = jnp.zeros((TAPS, part), bf16)

        @pl.loop(chunk * tiles // CHUNKS, (chunk + 1) * tiles // CHUNKS)
        def _(tile):
            lanes = lanes_of(tile)
            fill_medium_table(table, adjoint_row, tile)
            for pair in range(blocks // 2):
                both = medium_pair(table, grad_conv, lanes, pair)
                for half in range(2):
                    rows = block_rows(2 * pair + half)
                    grad_input = both[:, LANES * half : LANES * (half + 1)]
                    stage1[rows, lanes] = (grad_input * value[rows, lanes].astype(f32)).astype(bf16)
                    stage2[rows, lanes] = (grad_input * key[rows, lanes].astype(f32)).astype(bf16)

        send_home(1, stage1, out1, chunk)
        send_home(2, stage2, out2, chunk)
        if chunk == 0:
            finish(sum_copies)
            y_sums[place.y] = core_sums[0] + core_sums[1]
            sum_copies = gather(y_sums, place.y, place.y_peers, sum_sems, 1)
        if chunk == 1:
            finish(sum_copies)
            x_sums[place.x] = sum(y_sums[s] for s in range(1, place.size_y)) + y_sums[0]
            sum_copies = gather(x_sums, place.x, place.x_peers, sum_sems, place.size_y)
    finish(sum_copies)
    summed = sum(x_sums[s] for s in range(1, place.size_x)) + x_sums[0]
    filter_out[...] = (
        jnp.dot(summed, flip, precision=highest, preferred_element_type=f32) * scale
    )

    for copy in cot_copies + tail_copies + head_copies:
        copy.wait_send()
    for copy in own_copies:
        copy.wait()
    finish(out_copies)


def on_device(
    sizes, grad_out, query_medium, key_medium, value_medium, query_modal, key_modal,
    medium_filter, modal_decay, modal_residue,
):
    row_count, channels = query_medium.shape
    blocks = row_count // NEAR
    groups, modes = modal_decay.shape
    devices = lax.axis_size("ctx")
    size_z = lax.axis_size("ch")
    size_x, size_y, _ = sizes
    output = jax.ShapeDtypeStruct(grad_out.shape, bf16)
    filter_output = jax.ShapeDtypeStruct((groups, TAPS), f32)
    scale = 1.0 / math.sqrt(row_count * devices * GS)
    decay_rows = modal_decay.reshape(groups * modes // LANES, LANES)
    residue_rows = modal_residue.reshape(groups * modes // LANES, LANES)
    data = pltpu.VMEM((row_count, channels), bf16)
    longer = pltpu.VMEM((row_count + TAPS, channels), bf16)
    states = pltpu.VMEM((blocks, modes, channels), f32)
    state = pltpu.VMEM((modes, channels), f32)
    half = (modes, channels // 2)
    joins = [pltpu.VMEM((n,) + half, f32) for n in (2, size_y, size_x, 2)]
    dma = pltpu.SemaphoreType.DMA
    square = (groups, TAPS)
    whole = pl.BlockSpec(memory_space=pl.ANY)
    local = pl.BlockSpec(memory_space=pltpu.VMEM)
    outs = pl.pallas_call(
        lambda *refs: whole_kernel(sizes, scale, *refs),
        in_specs=[whole] * 6 + [local] * 3,
        out_shape=(output,) * 5 + (filter_output,),
        out_specs=(whole,) * 5 + (local,),
        scratch_shapes=[data] * 6
        + [longer, pltpu.VMEM((row_count, channels), f32), data, longer]
        + [data] * 5
        + [states] * 2 + [state] * 5
        + joins * 2
        + [pltpu.VMEM((groups, 2 * TAPS), f32)] * 2
        + [pltpu.VMEM((TILE_GROUPS * NEAR, 2 * NEAR), bf16),
           pltpu.VMEM((2 * NEAR, blocks * LANES), bf16),
           pltpu.VMEM((TILE_GROUPS * NEAR, blocks * LANES), bf16)]
        + [pltpu.VMEM(square, f32)]
        + [pltpu.VMEM((n,) + square, f32) for n in (2, size_y, size_x)]
        + [dma((5,))] + [dma((size_z - 1, CHUNKS))] * 2 + [dma((CHUNKS,))] * 4
        + [dma((size_x + size_y,))] * 4 + [dma((size_x + size_y,))] * 2
        + [dma((5, size_z - 1, CHUNKS))] * 2 + [dma((6,))],
        compiler_params=pltpu.CompilerParams(
            collective_id=0, has_side_effects=True, vmem_limit_bytes=60 * 1024 * 1024
        ),
    )(
        grad_out, query_medium, key_medium, value_medium, query_modal, key_modal,
        medium_filter, decay_rows, residue_rows,
    )
    return tuple(outs)


def solution(mesh):
    count = mesh.shape["ctx"] // 2
    side = math.isqrt(count)
    sizes = (side, count // side, 2)

    def body(*args):
        return on_device(sizes, *args)

    rows = P(("ctx", "ch"), None)
    groups = P("ch", None)
    return jax.shard_map(
        body,
        mesh=mesh,
        in_specs=(rows,) + (P("ctx", "ch"),) * 5 + (groups,) * 3,
        out_specs=(rows,) * 5 + (groups,),
        check_vma=False,
    )
```

time: 634 us -> 177 us (0.28); the launches traced: 623 us -> 177 us
  local copies, waits for them, and re-layouts: 266 us -> 15.2 us
  Pallas kernels: 0 us -> 161 us
  waiting for transfers between devices: 130 us -> 0 us
  other arithmetic: 113 us -> 0 us
  matrix products: 62.8 us -> 0 us
  starting transfers between devices: 35.6 us -> 0 us
  between operations: 14.5 us -> 0.66 us
    pallas_call x0 -> x1, Pallas kernels: none -> 161 us  [on_device(): pl.pallas_call(lambda *refs: whole_kernel(sizes, scale, *refs), in_specs=...]
    psum x1 -> x0, waiting for transfers between devices: 101 us -> none  [on_device(): grad_medium_filter = lax.psum(filter_partial, 'ctx') * filter_scale]
    select_n x62 -> x0, other arithmetic: 66.4 us -> none  [lap(): jnp.where(position < mine, new, old)]
    reshape x9 -> x2, local copies, waits for them, and re-layouts: 64.4 us -> 1.37 us  [the longest x1 0.68 us: on_device(): decay_rows = modal_decay.reshape(groups * modes // LANES, LANES)]
    dot_general x12 -> x0, matrix products: 62.8 us -> none  [the longest x1 7.84 us: medium_apply(): jnp.einsum('gcbs,grs->gcbr', column_blocks(current_cols, TAPS), curr_tab,...]
    unnamed x66 -> x18, local copies, waits for them, and re-layouts: 68.7 us -> 13.8 us
    concatenate x7 -> x0, local copies, waits for them, and re-layouts: 31.2 us -> none  [the longest x1 17.6 us: medium_products(): return jnp.concatenate([front_part, back_part], axis=2)]
    all_to_all x6 -> x0, waiting for transfers between devices: 28.3 us -> none  [the longest x1 20.5 us: on_device(): lax.all_to_all(grad_out, 'ch', split_axis=1, concat_axis=0, tiled=True)]
  transfers between devices with their start and end apart: 12 -> 0, of which waited for: 4 -> 0; matrix products, arithmetic and copies ran while one was open for 56% -> 0% of each run, Pallas kernels for 0% -> 0%
where the time goes in v2:
time: 177 us
  Pallas kernels  161 us (91%)
  local copies, waits for them, and re-layouts  15.2 us (9%)
    pallas_call x1, Pallas kernels, on_device(): pl.pallas_call(lambda *refs: whole_kernel(sizes, scale, *refs), in_specs=...  161 us
    unnamed x18, local copies, waits for them, and re-layouts  13.8 us

profile of v2, /device:TPU:1, one launch (start us, length us, event | category | flops | bytes accessed | tf_op | source)
XLA Modules:
  0.0 176.6 jit_solution(11785283254767618283)
XLA Ops:
  0.6 0.8 copy.17
  1.4 0.7 reshape.18.refs_7_
  2.1 0.8 copy.18
  2.9 0.7 reshape.19.refs_8_
  3.6 160.7 %shard_map.136 = (bf16[128,8192]{1,0:T(8,128)(2,1)}, bf16[128,8192]{1,0:T(8,128)(2,1)}, bf16[128,8192]{1,0:T(8,128)(2,1)}, bf16[128,8192]{1,0:T(8,128)(2,1)}, bf...) custom-call(bf16[128,8192]{1,0:T(8,128)(2,1)} %refs_0_.1, bf16[512,2048]{1,0:T(8,128)(2,1)} %refs_1_.1, ...), custom_call_target="tpu_custom_call" | custom-call | tf_op jit(solution)/shard_map/pallas_call | solution.py:611
  164.3 0.0 copy-start.3
  164.3 3.2 %copy.25 = bf16[128,8192]{1,0:T(8,128)(2,1)} copy(bf16[128,8192]{1,0:T(8,128)(2,1)} %get-tuple-element.12) | data formatting | bytes 4194304
  167.6 0.0 copy-done.3
  167.6 0.0 copy-start.2
  167.6 1.3 copy.26
  168.9 1.0 copy-done.2
  169.9 0.0 copy-start.1
  169.9 1.3 copy.27
  171.2 1.0 copy-done.1
  172.3 0.0 copy-start
  172.3 1.3 copy.28
  173.6 1.0 copy-done
  174.6 0.0 copy-start.4
  174.6 1.3 copy.29
  175.9 0.0 copy-done.4
  175.9 0.6 copy.30
Async XLA Ops:
  164.3 3.3 %copy-start.3 = (bf16[128,8192]{1,0:T(8,128)(2,1)S(1)}, bf16[128,8192]{1,0:T(8,128)(2,1)}, u32[]{:S(2)}) copy-start(bf16[128,8192]{1,0:T(8,128)(2,1)} %get-tuple-element.13) | copy-start | bytes 6291460
  167.6 2.3 %copy-start.2 = (bf16[128,8192]{1,0:T(8,128)(2,1)S(1)}, bf16[128,8192]{1,0:T(8,128)(2,1)}, u32[]{:S(2)}) copy-start(bf16[128,8192]{1,0:T(8,128)(2,1)} %get-tuple-element.14) | copy-start | bytes 6291460
  169.9 2.3 %copy-start.1 = (bf16[128,8192]{1,0:T(8,128)(2,1)S(1)}, bf16[128,8192]{1,0:T(8,128)(2,1)}, u32[]{:S(2)}) copy-start(bf16[128,8192]{1,0:T(8,128)(2,1)} %get-tuple-element.15) | copy-start | bytes 6291460
  172.3 2.3 %copy-start = (bf16[128,8192]{1,0:T(8,128)(2,1)S(1)}, bf16[128,8192]{1,0:T(8,128)(2,1)}, u32[]{:S(2)}) copy-start(bf16[128,8192]{1,0:T(8,128)(2,1)} %get-tuple-element.16) | copy-start | bytes 6291460
  174.6 1.3 copy-start.4

commit v3 on v2

--- a/solution.py
+++ b/solution.py
@@ -175,13 +175,15 @@
 
 
 class Join:
-    def __init__(self, place, forward, total_ref, result_ref, log_ref, pair, by_y, by_x, out, sems):
+    def __init__(
+        self, place, forward, low, width, total_ref, result_ref, log_ref, pair, by_y, by_x, out, sems
+    ):
         self.place, self.forward = place, forward
         self.total, self.result, self.log = total_ref, result_ref, log_ref
         self.pair, self.by_y, self.by_x, self.out, self.sems = pair, by_y, by_x, out, sems
-        half = total_ref.shape[1] // 2
-        self.mine = pl.ds(pl.multiple_of(place.core * half, half), half)
-        self.other = pl.ds(pl.multiple_of((1 - place.core) * half, half), half)
+        half = width // 2
+        self.mine = pl.ds(pl.multiple_of(low + place.core * half, half), half)
+        self.other = pl.ds(pl.multiple_of(low + (1 - place.core) * half, half), half)
         self.span = 4 * NEAR
 
     def decay(self, steps):
@@ -256,10 +258,10 @@
     medium_input, conv, medium_out, grad_conv,
     stage0, stage1, stage2, stage3, stage4,
     end_states, start_states, own_total, own_adjoint, entering, arriving, log_rows,
-    pair_f, y_f, x_f, o_f, pair_b, y_b, x_b, o_b,
-    forward_row, adjoint_row, table, wide, left, sums, core_sums, y_sums, x_sums,
+    pair_f, y_f, x_f, o_f, pair_s, y_s, x_s, o_s, pair_b, y_b, x_b, o_b,
+    decay_rows, residue_rows, forward_row, adjoint_row, table, wide, left, sums, core_sums, y_sums, x_sums,
     load_sem, cot_send, cot_recv, tail_send, tail_recv, head_send, head_recv,
-    join_send, join_recv, back_send, back_recv, sum_send, sum_recv,
+    join_send, join_recv, join2_send, join2_recv, back_send, back_recv, sum_send, sum_recv,
     out_send, out_recv, own_sem,
 ):
     place = Place(sizes)
@@ -269,7 +271,7 @@
     row_count, channels = query.shape
     blocks = row_count // NEAR
     tiles = channels // LANES
-    modes = own_total.shape[0]
+    modes, groups = decay_ref.shape
     part = channels // CHUNKS
     following = lax.rem(me + 1, devices)
     previous = lax.rem(me + devices - 1, devices)
@@ -337,9 +339,6 @@
     adjoint_row[:, 0:TAPS] = taps_in.astype(f32)
     adjoint_row[:, TAPS:] = jnp.zeros(taps_in.shape, f32)
     wide[NEAR + 3 * modes :] = jnp.zeros((NEAR - 3 * modes, wide.shape[1]), bf16)
-    spread = jnp.where(
-        lax.shift_right_logical(ramp(0), 4) == lax.shift_right_logical(ramp(1), 4), 1.0, 0.0
-    )
     own_mode = jnp.bitwise_and(iota((modes, LANES), 1), modes - 1) == iota((modes, LANES), 0)
 
     def lanes_of(tile):
@@ -347,16 +346,28 @@
 
     @pl.loop(0, tiles)
     def _(tile):
-        kept = jnp.where(own_mode, decay_ref[pl.ds(tile, 1)], 0.0)
-        log_rows[:, lanes_of(tile)] = jnp.log(
-            jnp.dot(kept, spread, precision=highest, preferred_element_type=f32)
-        )
+        spread = jnp.where(
+            iota((groups, LANES), 0)
+            == tile * TILE_GROUPS + lax.shift_right_logical(iota((groups, LANES), 1), 4),
+            1.0, 0.0,
+        )
+
+        def per_channel(ref):
+            return jnp.dot(ref[...], spread, precision=highest, preferred_element_type=f32)
+
+        def per_mode(value):
+            return jnp.sum(jnp.where(own_mode, value, 0.0), axis=0, keepdims=True)
+
+        decay = per_channel(decay_ref)
+        log_rows[:, lanes_of(tile)] = jnp.log(decay)
+        decay_rows[pl.ds(tile, 1)] = per_mode(decay)
+        residue_rows[pl.ds(tile, 1)] = per_mode(per_channel(residue_ref))
 
     loads[2].wait()
     loads[3].wait()
     early = slice(0, row_count - TAPS)
 
-    for chunk in range(CHUNKS):
+    def medium_forward(chunk):
         tail_copies[chunk].wait_recv()
 
         @pl.when(me == 0)
@@ -378,7 +389,7 @@
                     out = (query[rows, lanes].astype(f32) * part_conv).astype(bf16)
                     medium_out[rows, lanes] = out
                     inputs.append(product(key_modal[rows, lanes], out))
-            log_row = jnp.log(decay_ref[pl.ds(tile, 1)])
+            log_row = jnp.log(decay_rows[pl.ds(tile, 1)])
             weight = jnp.exp(log_row * (NEAR - 1 - ramp(0)).astype(f32))
             states = block_states(weight, jnp.concatenate(inputs, axis=1))
             step = jnp.exp(log_rows[:, lanes] * NEAR)
@@ -389,15 +400,6 @@
                 total = step * total + state
             own_total[:, lanes] = total
 
-    forward = Join(place, True, own_total, entering, log_rows, pair_f, y_f, x_f, o_f,
-                   (join_send, join_recv))
-    backward = Join(place, False, own_adjoint, arriving, log_rows, pair_b, y_b, x_b, o_b,
-                    (back_send, back_recv))
-    forward.start()
-    cot_own.wait()
-    loads[4].wait()
-    forward.along_y()
-
     def adjoint_states(chunk):
         for copy in cot_copies[(size_z - 1) * chunk : (size_z - 1) * (chunk + 1)]:
             copy.wait_recv()
@@ -410,7 +412,7 @@
                  for b in range(blocks)],
                 axis=1,
             )
-            log_row = jnp.log(decay_ref[pl.ds(tile, 1)])
+            log_row = jnp.log(decay_rows[pl.ds(tile, 1)])
             states = block_states(jnp.exp(log_row * ramp(0).astype(f32)), grads)
             step = jnp.exp(log_rows[:, lanes] * NEAR)
             total = jnp.zeros((modes, LANES), f32)
@@ -419,15 +421,6 @@
                 start_states[b, :, lanes] = state
                 total = step * total + state
             own_adjoint[:, lanes] = total
-
-    adjoint_states(0)
-    adjoint_states(1)
-    forward.along_x()
-    adjoint_states(2)
-    adjoint_states(3)
-    forward.share()
-    backward.start()
-    forward.end()
 
     out_copies, own_copies = [], []
 
@@ -448,13 +441,12 @@
             copy.start()
             own_copies.append(copy)
 
-    for chunk in range(CHUNKS):
-
+    def modal_forward(chunk):
         @pl.loop(chunk * tiles // CHUNKS, (chunk + 1) * tiles // CHUNKS)
         def _(tile):
             lanes = lanes_of(tile)
-            log_row = jnp.log(decay_ref[pl.ds(tile, 1)])
-            fill_modal_table(table, log_row, residue_ref[pl.ds(tile, 1)], modes, False)
+            log_row = jnp.log(decay_rows[pl.ds(tile, 1)])
+            fill_modal_table(table, log_row, residue_rows[pl.ds(tile, 1)], modes, False)
             step = jnp.exp(log_rows[:, lanes] * NEAR)
             carried = entering[:, lanes]
             befores = []
@@ -470,12 +462,42 @@
                 stage3[rows, lanes] = (cotangent[rows, lanes].astype(f32) * parts[b]).astype(bf16)
 
         send_home(3, stage3, out3, chunk)
-        if chunk == 0:
-            backward.along_y()
-        if chunk == 1:
-            backward.along_x()
-        if chunk == 2:
-            backward.share()
+
+    half = channels // 2
+    first = Join(place, True, 0, half, own_total, entering, log_rows, pair_f, y_f, x_f, o_f,
+                 (join_send, join_recv))
+    second = Join(place, True, half, half, own_total, entering, log_rows, pair_s, y_s, x_s, o_s,
+                  (join2_send, join2_recv))
+    backward = Join(place, False, 0, channels, own_adjoint, arriving, log_rows,
+                    pair_b, y_b, x_b, o_b, (back_send, back_recv))
+    medium_forward(0)
+    medium_forward(1)
+    first.start()
+    medium_forward(2)
+    first.along_y()
+    medium_forward(3)
+    second.start()
+    first.along_x()
+    cot_own.wait()
+    loads[4].wait()
+    adjoint_states(0)
+    second.along_y()
+    first.share()
+    adjoint_states(1)
+    second.along_x()
+    first.end()
+    modal_forward(0)
+    second.share()
+    modal_forward(1)
+    second.end()
+    adjoint_states(2)
+    adjoint_states(3)
+    backward.start()
+    modal_forward(2)
+    backward.along_y()
+    modal_forward(3)
+    backward.along_x()
+    backward.share()
     backward.end()
 
     head_copies = []
@@ -484,8 +506,8 @@
         @pl.loop(chunk * tiles // CHUNKS, (chunk + 1) * tiles // CHUNKS)
         def _(tile):
             lanes = lanes_of(tile)
-            log_row = jnp.log(decay_ref[pl.ds(tile, 1)])
-            fill_modal_table(table, log_row, residue_ref[pl.ds(tile, 1)], modes, True)
+            log_row = jnp.log(decay_rows[pl.ds(tile, 1)])
+            fill_modal_table(table, log_row, residue_rows[pl.ds(tile, 1)], modes, True)
             step = jnp.exp(log_rows[:, lanes] * NEAR)
             carried = arriving[:, lanes]
             nexts = [carried] * blocks
@@ -583,6 +605,18 @@
     finish(out_copies)
 
 
+def store_kernel(*refs):
+    sems = refs[-1]
+    count = (len(refs) - 1) // 2
+    copies = [
+        pltpu.make_async_copy(refs[n], refs[count + n], sems.at[n]) for n in range(count)
+    ]
+    for copy in copies:
+        copy.start()
+    for copy in copies:
+        copy.wait()
+
+
 def on_device(
     sizes, grad_out, query_medium, key_medium, value_medium, query_modal, key_modal,
     medium_filter, modal_decay, modal_residue,
@@ -596,14 +630,14 @@
     output = jax.ShapeDtypeStruct(grad_out.shape, bf16)
     filter_output = jax.ShapeDtypeStruct((groups, TAPS), f32)
     scale = 1.0 / math.sqrt(row_count * devices * GS)
-    decay_rows = modal_decay.reshape(groups * modes // LANES, LANES)
-    residue_rows = modal_residue.reshape(groups * modes // LANES, LANES)
     data = pltpu.VMEM((row_count, channels), bf16)
     longer = pltpu.VMEM((row_count + TAPS, channels), bf16)
     states = pltpu.VMEM((blocks, modes, channels), f32)
     state = pltpu.VMEM((modes, channels), f32)
-    half = (modes, channels // 2)
-    joins = [pltpu.VMEM((n,) + half, f32) for n in (2, size_y, size_x, 2)]
+
+    def joins(width):
+        return [pltpu.VMEM((n, modes, width // 2), f32) for n in (2, size_y, size_x, 2)]
+
     dma = pltpu.SemaphoreType.DMA
     square = (groups, TAPS)
     whole = pl.BlockSpec(memory_space=pl.ANY)
@@ -611,13 +645,14 @@
     outs = pl.pallas_call(
         lambda *refs: whole_kernel(sizes, scale, *refs),
         in_specs=[whole] * 6 + [local] * 3,
-        out_shape=(output,) * 5 + (filter_output,),
-        out_specs=(whole,) * 5 + (local,),
+        out_shape=(pltpu.VMEM(grad_out.shape, bf16),) * 5 + (filter_output,),
+        out_specs=(local,) * 6,
         scratch_shapes=[data] * 6
         + [longer, pltpu.VMEM((row_count, channels), f32), data, longer]
         + [data] * 5
         + [states] * 2 + [state] * 5
-        + joins * 2
+        + joins(channels // 2) * 2 + joins(channels)
+        + [pltpu.VMEM((groups * modes // LANES, LANES), f32)] * 2
         + [pltpu.VMEM((groups, 2 * TAPS), f32)] * 2
         + [pltpu.VMEM((TILE_GROUPS * NEAR, 2 * NEAR), bf16),
            pltpu.VMEM((2 * NEAR, blocks * LANES), bf16),
@@ -625,16 +660,24 @@
         + [pltpu.VMEM(square, f32)]
         + [pltpu.VMEM((n,) + square, f32) for n in (2, size_y, size_x)]
         + [dma((5,))] + [dma((size_z - 1, CHUNKS))] * 2 + [dma((CHUNKS,))] * 4
-        + [dma((size_x + size_y,))] * 4 + [dma((size_x + size_y,))] * 2
+        + [dma((size_x + size_y,))] * 6 + [dma((size_x + size_y,))] * 2
         + [dma((5, size_z - 1, CHUNKS))] * 2 + [dma((6,))],
         compiler_params=pltpu.CompilerParams(
-            collective_id=0, has_side_effects=True, vmem_limit_bytes=60 * 1024 * 1024
+            collective_id=0, has_side_effects=True, vmem_limit_bytes=48 * 1024 * 1024
         ),
     )(
         grad_out, query_medium, key_medium, value_medium, query_modal, key_modal,
-        medium_filter, decay_rows, residue_rows,
+        medium_filter, modal_decay.T, modal_residue.T,
     )
-    return tuple(outs)
+    stored = pl.pallas_call(
+        store_kernel,
+        in_specs=[local] * 5,
+        out_shape=(output,) * 5,
+        out_specs=(whole,) * 5,
+        scratch_shapes=[dma((5,))],
+        compiler_params=pltpu.CompilerParams(vmem_limit_bytes=2 * 1024 * 1024),
+    )(*[pltpu.with_memory_space_constraint(out, pltpu.VMEM) for out in outs[:5]])
+    return tuple(stored) + (outs[5],)
 
 
 def solution(mesh):

time: 177 us -> 164 us (0.927)
  local copies, waits for them, and re-layouts: 15.2 us -> 0.64 us
    unnamed x18 -> x3, local copies, waits for them, and re-layouts: 13.8 us -> 0.64 us
    pallas_call x0 -> x1, Pallas kernels: none -> 4.01 us  [on_device(): pl.pallas_call(store_kernel, in_specs=[local] * 5, out_shape=(output,) *...]
    pallas_call x1, Pallas kernels: 161 us -> 158 us  [on_device(): pl.pallas_call(lambda *refs: whole_kernel(sizes, scale, *refs), in_specs=...]
where the time goes in v3:
time: 164 us
  Pallas kernels  162 us (99%)
    pallas_call x1, Pallas kernels, on_device(): pl.pallas_call(lambda *refs: whole_kernel(sizes, scale, *refs), in_specs=...  158 us
    pallas_call x1, Pallas kernels, on_device(): pl.pallas_call(store_kernel, in_specs=[local] * 5, out_shape=(output,) *...  4.01 us

profile of v3, /device:TPU:1, one launch (start us, length us, event | category | flops | bytes accessed | tf_op | source)
XLA Modules:
  0.0 163.5 jit_solution(14501743137803998125)
XLA Ops:
  0.6 158.2 %shard_map.136 = (bf16[128,8192]{1,0:T(8,128)(2,1)S(1)}, bf16[128,8192]{1,0:T(8,128)(2,1)S(1)}, bf16[128,8192]{1,0:T(8,128)(2,1)S(1)}, bf16[128,8192]{1,0:T(8,12...) custom-call(bf16[128,8192]{1,0:T(8,128)(2,1)} %refs_0_.1, bf16[512,2048]{1,0:T(8,128)(2,1)} %refs_1_.1, ...), custom_call_target="tpu_custom_call" | custom-call | tf_op jit(solution)/shard_map/pallas_call | solution.py:645
  158.9 0.0 copy-start
  158.9 4.0 %shard_map.137 = (bf16[128,8192]{1,0:T(8,128)(2,1)}, bf16[128,8192]{1,0:T(8,128)(2,1)}, bf16[128,8192]{1,0:T(8,128)(2,1)}, bf16[128,8192]{1,0:T(8,128)(2,1)}, bf16[128,8192]{1,0:T(8,128)(2,1)}) custom-call(bf16[128,8192]{1,0:T(8,128)(2,1)S(1)} %get-tuple-element.17.refs_0_, bf16[128,8192]{1,0:T(8,128)(2,1)S(1)} %get-tuple-element.18.refs_1_, ...), custom_call_target="tpu_custom_call" | custom-call | tf_op jit(solution)/shard_map/pallas_call | solution.py:672
  162.9 0.0 copy-done
  162.9 0.6 copy.16
Async XLA Ops:
  158.9 4.0 %copy-start = (f32[128,128]{1,0:T(8,128)S(1)}, f32[128,128]{1,0:T(8,128)}, u32[]{:S(2)}) copy-start(f32[128,128]{1,0:T(8,128)} %get-tuple-element.39) | copy-start | bytes 196612

commit v4 on v3

--- a/solution.py
+++ b/solution.py
@@ -12,7 +12,8 @@
 NEAR = 128
 LANES = 128
 TILE_GROUPS = LANES // GS
-CHUNKS = 4
+BOUNDS = (0, 2, 6, 9, 12, 16)
+CHUNKS = len(BOUNDS) - 1
 MESH = pl.DeviceIdType.MESH
 
 f32 = jnp.float32
@@ -182,8 +183,8 @@
         self.total, self.result, self.log = total_ref, result_ref, log_ref
         self.pair, self.by_y, self.by_x, self.out, self.sems = pair, by_y, by_x, out, sems
         half = width // 2
-        self.mine = pl.ds(pl.multiple_of(low + place.core * half, half), half)
-        self.other = pl.ds(pl.multiple_of(low + (1 - place.core) * half, half), half)
+        self.mine = pl.ds(pl.multiple_of(low + place.core * half, LANES), half)
+        self.other = pl.ds(pl.multiple_of(low + (1 - place.core) * half, LANES), half)
         self.span = 4 * NEAR
 
     def decay(self, steps):
@@ -272,12 +273,19 @@
     blocks = row_count // NEAR
     tiles = channels // LANES
     modes, groups = decay_ref.shape
-    part = channels // CHUNKS
+    edges = [tiles * bound // BOUNDS[-1] for bound in BOUNDS]
     following = lax.rem(me + 1, devices)
     previous = lax.rem(me + devices - 1, devices)
 
+    def width(chunk):
+        return (edges[chunk + 1] - edges[chunk]) * LANES
+
     def columns(chunk):
-        return pl.ds(chunk * part, part)
+        return pl.ds(edges[chunk] * LANES, width(chunk))
+
+    def columns_of(owner, chunk):
+        start = owner * channels + edges[chunk] * LANES
+        return pl.ds(pl.multiple_of(start, LANES), width(chunk))
 
     loads = [
         pltpu.make_async_copy(source, target, load_sem.at[n])
@@ -304,7 +312,7 @@
     cot_copies = []
     for chunk in range(CHUNKS):
         for k, peer in enumerate(z_peers):
-            source = pl.ds(pl.multiple_of(peer * channels + chunk * part, part), part)
+            source = columns_of(peer, chunk)
             copy = remote(
                 cotangent_in.at[:, source], cotangent.at[own_rows, columns(chunk)],
                 (cot_send.at[k], cot_recv.at[k]), chunk, {"ch": peer},
@@ -372,9 +380,9 @@
 
         @pl.when(me == 0)
         def _():
-            medium_input[0:TAPS, columns(chunk)] = jnp.zeros((TAPS, part), bf16)
-
-        @pl.loop(chunk * tiles // CHUNKS, (chunk + 1) * tiles // CHUNKS)
+            medium_input[0:TAPS, columns(chunk)] = jnp.zeros((TAPS, width(chunk)), bf16)
+
+        @pl.loop(edges[chunk], edges[chunk + 1])
         def _(tile):
             lanes = lanes_of(tile)
             medium_input[TAPS:row_count, lanes] = product(key[early, lanes], value[early, lanes])
@@ -404,7 +412,7 @@
         for copy in cot_copies[(size_z - 1) * chunk : (size_z - 1) * (chunk + 1)]:
             copy.wait_recv()
 
-        @pl.loop(chunk * tiles // CHUNKS, (chunk + 1) * tiles // CHUNKS)
+        @pl.loop(edges[chunk], edges[chunk + 1])
         def _(tile):
             lanes = lanes_of(tile)
             grads = jnp.concatenate(
@@ -427,7 +435,7 @@
     def send_home(n, stage, out, chunk):
         for k, peer in enumerate(z_peers):
             rows = pl.ds(pl.multiple_of(peer * NEAR, NEAR), NEAR)
-            target = pl.ds(pl.multiple_of(z * channels + chunk * part, part), part)
+            target = columns_of(z, chunk)
             copy = remote(
                 stage.at[rows, columns(chunk)], out.at[:, target],
                 (out_send.at[n, k], out_recv.at[n, k]), chunk, {"ch": peer},
@@ -442,7 +450,7 @@
             own_copies.append(copy)
 
     def modal_forward(chunk):
-        @pl.loop(chunk * tiles // CHUNKS, (chunk + 1) * tiles // CHUNKS)
+        @pl.loop(edges[chunk], edges[chunk + 1])
         def _(tile):
             lanes = lanes_of(tile)
             log_row = jnp.log(decay_rows[pl.ds(tile, 1)])
@@ -463,11 +471,11 @@
 
         send_home(3, stage3, out3, chunk)
 
-    half = channels // 2
-    first = Join(place, True, 0, half, own_total, entering, log_rows, pair_f, y_f, x_f, o_f,
-                 (join_send, join_recv))
-    second = Join(place, True, half, half, own_total, entering, log_rows, pair_s, y_s, x_s, o_s,
-                  (join2_send, join2_recv))
+    early_width = edges[2] * LANES
+    first = Join(place, True, 0, early_width, own_total, entering, log_rows,
+                 pair_f, y_f, x_f, o_f, (join_send, join_recv))
+    second = Join(place, True, early_width, channels - early_width, own_total, entering, log_rows,
+                  pair_s, y_s, x_s, o_s, (join2_send, join2_recv))
     backward = Join(place, False, 0, channels, own_adjoint, arriving, log_rows,
                     pair_b, y_b, x_b, o_b, (back_send, back_recv))
     medium_forward(0)
@@ -476,34 +484,37 @@
     medium_forward(2)
     first.along_y()
     medium_forward(3)
+    first.along_x()
+    medium_forward(4)
     second.start()
-    first.along_x()
+    first.share()
     cot_own.wait()
     loads[4].wait()
     adjoint_states(0)
     second.along_y()
-    first.share()
     adjoint_states(1)
-    second.along_x()
     first.end()
     modal_forward(0)
+    second.along_x()
+    modal_forward(1)
     second.share()
-    modal_forward(1)
-    second.end()
     adjoint_states(2)
     adjoint_states(3)
+    adjoint_states(4)
     backward.start()
+    second.end()
     modal_forward(2)
     backward.along_y()
     modal_forward(3)
     backward.along_x()
+    modal_forward(4)
     backward.share()
     backward.end()
 
     head_copies = []
     for chunk in range(CHUNKS):
 
-        @pl.loop(chunk * tiles // CHUNKS, (chunk + 1) * tiles // CHUNKS)
+        @pl.loop(edges[chunk], edges[chunk + 1])
         def _(tile):
             lanes = lanes_of(tile)
             log_row = jnp.log(decay_rows[pl.ds(tile, 1)])
@@ -568,9 +579,9 @@
 
         @pl.when(me == devices - 1)
         def _():
-            grad_conv[row_count:, columns(chunk)] = jnp.zeros((TAPS, part), bf16)
-
-        @pl.loop(chunk * tiles // CHUNKS, (chunk + 1) * tiles // CHUNKS)
+            grad_conv[row_count:, columns(chunk)] = jnp.zeros((TAPS, width(chunk)), bf16)
+
+        @pl.loop(edges[chunk], edges[chunk + 1])
         def _(tile):
             lanes = lanes_of(tile)
             fill_medium_table(table, adjoint_row, tile)
@@ -635,6 +646,8 @@
     states = pltpu.VMEM((blocks, modes, channels), f32)
     state = pltpu.VMEM((modes, channels), f32)
 
+    early_width = channels * BOUNDS[2] // BOUNDS[-1]
+
     def joins(width):
         return [pltpu.VMEM((n, modes, width // 2), f32) for n in (2, size_y, size_x, 2)]
 
@@ -651,7 +664,7 @@
         + [longer, pltpu.VMEM((row_count, channels), f32), data, longer]
         + [data] * 5
         + [states] * 2 + [state] * 5
-        + joins(channels // 2) * 2 + joins(channels)
+        + joins(early_width) + joins(channels - early_width) + joins(channels)
         + [pltpu.VMEM((groups * modes // LANES, LANES), f32)] * 2
         + [pltpu.VMEM((groups, 2 * TAPS), f32)] * 2
         + [pltpu.VMEM((TILE_GROUPS * NEAR, 2 * NEAR), bf16),

time: 164 us -> 158 us (0.963)
  Pallas kernels: 162 us -> 156 us
    pallas_call x1, Pallas kernels: 158 us -> 152 us  [on_device(): pl.pallas_call(lambda *refs: whole_kernel(sizes, scale, *refs), in_specs=...]
where the time goes in v4:
time: 158 us
  Pallas kernels  156 us (99%)
    pallas_call x1, Pallas kernels, on_device(): pl.pallas_call(lambda *refs: whole_kernel(sizes, scale, *refs), in_specs=...  152 us
    pallas_call x1, Pallas kernels, on_device(): pl.pallas_call(store_kernel, in_specs=[local] * 5, out_shape=(output,) *...  4.01 us

profile of v4, /device:TPU:1, one launch (start us, length us, event | category | flops | bytes accessed | tf_op | source)
XLA Modules:
  0.0 157.7 jit_solution(5485366485089156954)
XLA Ops:
  0.6 152.4 %shard_map.136 = (bf16[128,8192]{1,0:T(8,128)(2,1)S(1)}, bf16[128,8192]{1,0:T(8,128)(2,1)S(1)}, bf16[128,8192]{1,0:T(8,128)(2,1)S(1)}, bf16[128,8192]{1,0:T(8,12...) custom-call(bf16[128,8192]{1,0:T(8,128)(2,1)} %refs_0_.1, bf16[512,2048]{1,0:T(8,128)(2,1)} %refs_1_.1, ...), custom_call_target="tpu_custom_call" | custom-call | tf_op jit(solution)/shard_map/pallas_call | solution.py:658
  153.1 0.0 copy-start
  153.1 4.0 %shard_map.137 = (bf16[128,8192]{1,0:T(8,128)(2,1)}, bf16[128,8192]{1,0:T(8,128)(2,1)}, bf16[128,8192]{1,0:T(8,128)(2,1)}, bf16[128,8192]{1,0:T(8,128)(2,1)}, bf16[128,8192]{1,0:T(8,128)(2,1)}) custom-call(bf16[128,8192]{1,0:T(8,128)(2,1)S(1)} %get-tuple-element.17.refs_0_, bf16[128,8192]{1,0:T(8,128)(2,1)S(1)} %get-tuple-element.18.refs_1_, ...), custom_call_target="tpu_custom_call" | custom-call | tf_op jit(solution)/shard_map/pallas_call | solution.py:685
  157.1 0.0 copy-done
  157.1 0.6 copy.16
Async XLA Ops:
  153.1 4.0 %copy-start = (f32[128,128]{1,0:T(8,128)S(1)}, f32[128,128]{1,0:T(8,128)}, u32[]{:S(2)}) copy-start(f32[128,128]{1,0:T(8,128)} %get-tuple-element.39) | copy-start | bytes 196612

commit v5 on v4

--- a/solution.py
+++ b/solution.py
@@ -658,7 +658,7 @@
     outs = pl.pallas_call(
         lambda *refs: whole_kernel(sizes, scale, *refs),
         in_specs=[whole] * 6 + [local] * 3,
-        out_shape=(pltpu.VMEM(grad_out.shape, bf16),) * 5 + (filter_output,),
+        out_shape=(pltpu.VMEM(grad_out.shape, bf16),) * 5 + (pltpu.VMEM((groups, TAPS), f32),),
         out_specs=(local,) * 6,
         scratch_shapes=[data] * 6
         + [longer, pltpu.VMEM((row_count, channels), f32), data, longer]
@@ -684,13 +684,13 @@
     )
     stored = pl.pallas_call(
         store_kernel,
-        in_specs=[local] * 5,
-        out_shape=(output,) * 5,
-        out_specs=(whole,) * 5,
-        scratch_shapes=[dma((5,))],
+        in_specs=[local] * 6,
+        out_shape=(output,) * 5 + (filter_output,),
+        out_specs=(whole,) * 6,
+        scratch_shapes=[dma((6,))],
         compiler_params=pltpu.CompilerParams(vmem_limit_bytes=2 * 1024 * 1024),
-    )(*[pltpu.with_memory_space_constraint(out, pltpu.VMEM) for out in outs[:5]])
-    return tuple(stored) + (outs[5],)
+    )(*[pltpu.with_memory_space_constraint(out, pltpu.VMEM) for out in outs])
+    return tuple(stored)
 
 
 def solution(mesh):

time: 158 us -> 157 us (level)
  no operation moved by 1% of the time
where the time goes in v5:
time: 157 us
  Pallas kernels  156 us (99%)
    pallas_call x1, Pallas kernels, on_device(): pl.pallas_call(lambda *refs: whole_kernel(sizes, scale, *refs), in_specs=...  152 us
    pallas_call x1, Pallas kernels, on_device(): pl.pallas_call(store_kernel, in_specs=[local] * 6, out_shape=(output,) *...  4.02 us

profile of v5, /device:TPU:1, one launch (start us, length us, event | category | flops | bytes accessed | tf_op | source)
XLA Modules:
  0.0 156.7 jit_solution(6979402871259968323)
XLA Ops:
  0.6 151.8 %shard_map.136 = (bf16[128,8192]{1,0:T(8,128)(2,1)S(1)}, bf16[128,8192]{1,0:T(8,128)(2,1)S(1)}, bf16[128,8192]{1,0:T(8,128)(2,1)S(1)}, bf16[128,8192]{1,0:T(8,12...) custom-call(bf16[128,8192]{1,0:T(8,128)(2,1)} %refs_0_.1, bf16[512,2048]{1,0:T(8,128)(2,1)} %refs_1_.1, ...), custom_call_target="tpu_custom_call" | custom-call | tf_op jit(solution)/shard_map/pallas_call | solution.py:658
  152.5 4.0 %shard_map.137 = (bf16[128,8192]{1,0:T(8,128)(2,1)}, bf16[128,8192]{1,0:T(8,128)(2,1)}, bf16[128,8192]{1,0:T(8,128)(2,1)}, bf16[128,8192]{1,0:T(8,128)(2,1)}, bf...) custom-call(bf16[128,8192]{1,0:T(8,128)(2,1)S(1)} %get-tuple-element.12.refs_0_, ...), custom_call_target="tpu_custom_call" | custom-call | tf_op jit(solution)/shard_map/pallas_call | solution.py:685
